TPU v7x, 32 devices: a whole 2x2x4 slice. The times are simulated.
32 devices in a mesh: row: 8 (over z, x), col: 4 (over y, core).
Axes of the slice: x: 2, y: 2, z: 4, core: 2. Of those that a mesh axis runs over, the one named last changes fastest.
Arguments:
- excitation: bfloat16 [32768, 128], P(('row', 'col')), may hold values from -6 to 6
- near_list: int32 [256, 5], P(('row', 'col')), may hold values from 0 to 255, as said below
- near_blocks: bfloat16 [2, 32768, 640], P(None, ('row', 'col')), may hold values from -0.15625 to 0.15625
- col_factors: bfloat16 [2, 32768, 1024], P(None, ('row', 'col')), may hold values from -0.125 to 0.125
- coupling: bfloat16 [2, 16384, 1024], P(None, ('row', 'col')), may hold values from -0.125 to 0.125
- row_factors: bfloat16 [2, 32768, 512], P(None, ('row', 'col')), may hold values from -0.1875 to 0.1875
Outputs:
- response: bfloat16 [32768, 128], P(('row', 'col'))
Inputs may be any that keep to these rules, and one draw needn't show every extreme that they name: near_list[i, 0] = i; every entry lies within 8 leaves of i, and leaves at distance exactly 8 on either side occur.
All inputs are finite; a program needn't handle non-finite values.
Results may differ from a plain program's by a relative error of at most 0.008.
Values may be sent and summed in bfloat16 or wider, within the bound.
No kernel may reach another device: no remote copies, remote signals or barrier semaphores. Data moves between devices by JAX's collectives and lax.ppermute only.
A program may use at most 128 MiB of HBM per device.

v0:
```python
import jax
import jax.numpy as jnp
from jax import lax
from jax.sharding import PartitionSpec as P

RANK = 128
LEAF = 128
REACH = 8
NEAR = 5


def with_halo(cells, sides, width):
    for axis, dim in sides:
        count = lax.axis_size(axis)
        ends = count - 1
        head = lax.slice_in_dim(cells, 0, width, axis=dim)
        tail = lax.slice_in_dim(cells, cells.shape[dim] - width, cells.shape[dim], axis=dim)
        cells = jnp.concatenate(
            [
                lax.ppermute(tail, axis, [(i, (i + 1) % count) for i in range(ends)]),
                cells,
                lax.ppermute(head, axis, [((i + 1) % count, i) for i in range(ends)]),
            ],
            axis=dim,
        )
    return cells


def signed_swap(width):
    half = width // 2
    source = lax.broadcasted_iota(jnp.int32, (width, width), 0)
    target = lax.broadcasted_iota(jnp.int32, (width, width), 1)
    negative = jnp.where((target < half) & (source == target + half), -1.0, 0.0)
    positive = jnp.where((target >= half) & (source == target - half), 1.0, 0.0)
    return (negative + positive).astype(jnp.bfloat16)


def turn_flat(flat_data):
    rotation = signed_swap(flat_data.shape[1])
    return jnp.dot(flat_data, rotation, preferred_element_type=jnp.float32).astype(jnp.bfloat16)


def multiply_flat(real_part, imag_part, flat_data):
    turned = turn_flat(flat_data)
    summed = jnp.dot(real_part, flat_data, preferred_element_type=jnp.float32)
    return summed + jnp.dot(imag_part, turned, preferred_element_type=jnp.float32)


def project_flat(real_part, imag_part, flat_data):
    turned = turn_flat(flat_data)
    contract_dims = (((0,), (0,)), ((), ()))
    summed = lax.dot_general(
        real_part, flat_data, contract_dims, preferred_element_type=jnp.float32
    )
    return summed + lax.dot_general(
        imag_part, turned, contract_dims, preferred_element_type=jnp.float32
    )


def multiply_split_flat(real_part, imag_part, flat_data):
    upper_part = flat_data.astype(jnp.bfloat16)
    lower_part = (flat_data - upper_part.astype(jnp.float32)).astype(jnp.bfloat16)
    return multiply_flat(real_part, imag_part, upper_part) + multiply_flat(
        real_part, imag_part, lower_part
    )


def on_device(excitation, near_list, near_blocks, col_factors, coupling, row_factors):
    row_total = excitation.shape[0]
    width_cols = excitation.shape[1]
    leaves_here = row_total // LEAF
    row_count = lax.axis_size("row")
    col_count = lax.axis_size("col")
    padded = with_halo(excitation, ((("row", "col"), 0),), REACH * LEAF)
    leaves_pad = leaves_here + 2 * REACH
    table = padded.reshape(leaves_pad, LEAF * width_cols)
    first_leaf = lax.axis_index(("row", "col")) * leaves_here
    local_leaf = near_list - first_leaf + REACH
    slots = lax.broadcasted_iota(jnp.int32, (leaves_here, NEAR, leaves_pad), 2)
    selector = (
        (local_leaf[:, :, None] == slots)
        .astype(jnp.bfloat16)
        .reshape(leaves_here * NEAR, leaves_pad)
    )
    pieces = jnp.dot(selector, table, preferred_element_type=jnp.float32).astype(jnp.bfloat16)
    pieces = pieces.reshape(leaves_here * NEAR * LEAF, width_cols)
    turned = turn_flat(pieces).reshape(leaves_here, NEAR * LEAF, width_cols)
    pieces = pieces.reshape(leaves_here, NEAR * LEAF, width_cols)
    blocks_re = near_blocks[0].reshape(leaves_here, LEAF, NEAR * LEAF)
    blocks_im = near_blocks[1].reshape(leaves_here, LEAF, NEAR * LEAF)
    near_field = jnp.einsum("ilm,imc->ilc", blocks_re, pieces, preferred_element_type=jnp.float32)
    near_field = near_field + jnp.einsum(
        "ilm,imc->ilc", blocks_im, turned, preferred_element_type=jnp.float32
    )
    near_field = near_field.reshape(row_total, width_cols)
    compressed = project_flat(col_factors[0], col_factors[1], excitation)
    shaped = compressed.reshape(row_count, RANK, width_cols)
    arrived = lax.all_to_all(shaped, "row", split_axis=0, concat_axis=0, tiled=True)
    arrived_flat = arrived.reshape(row_count * RANK, width_cols)
    span_width = arrived_flat.shape[1]
    middle = multiply_split_flat(coupling[0], coupling[1], arrived_flat)
    middle = middle.reshape(col_count, RANK, span_width)
    landed = lax.all_to_all(middle, "col", split_axis=0, concat_axis=0, tiled=True)
    far_field = multiply_split_flat(
        row_factors[0], row_factors[1], landed.reshape(col_count * RANK, span_width)
    )
    return (near_field + far_field).astype(jnp.bfloat16)


def solution(mesh):
    return jax.shard_map(
        on_device,
        mesh=mesh,
        in_specs=(
            P(("row", "col"), None),
            P(("row", "col"), None),
            P(None, ("row", "col"), None),
            P(None, ("row", "col"), None),
            P(None, ("row", "col"), None),
            P(None, ("row", "col"), None),
        ),
        out_specs=P(("row", "col"), None),
        check_vma=False,
    )
```

profile of v0, /device:TPU:0, one launch (start us, length us, event | category | flops | bytes accessed | tf_op | source)
XLA Modules:
  0.0 59.9 jit_solution(2563850723202542655)
XLA Ops:
  0.0 1.4 %collective-permute-start.1 = (bf16[1024,128]{1,0:T(8,128)(2,1)}, bf16[1024,128]{1,0:T(8,128)(2,1)S(1)}, u32[]{:S(2)}, u32[]{:S(2)}) collective-permute-start(bf16[1024,128]{1,0:T(8,128)(2,1)} %param.6), channel_id=1, source_target_pairs={{1,0},{2,1},{3,2},{4,3},{5,4},{6,5},{7,6},{8,7},{9,8},{10,9},{11,1... | collective-permute-start | bytes 786440 | tf_op jit(solution)/shard_map/ppermute | solution.py:22
  1.4 3.1 %collective-permute-start = (bf16[1024,128]{1,0:T(8,128)(2,1)}, bf16[1024,128]{1,0:T(8,128)(2,1)S(1)}, u32[]{:S(2)}, u32[]{:S(2)}) collective-permute-start(bf16[1024,128]{1,0:T(8,128)(2,1)} %param.6), channel_id=1, source_target_pairs={{0,1},{1,2},{2,3},{3,4},{4,5},{5,6},{6,7},{7,8},{8,9},{9,10},{10,1... | collective-permute-start | bytes 786440 | tf_op jit(solution)/shard_map/ppermute | solution.py:20
  4.5 2.3 %fusion.2 = f32[1024,128]{1,0:T(8,128)S(1)} fusion(bf16[1024,128]{1,0:T(8,128)(2,1)} %param.6, bf16[2,1024,1024]{2,1,0:T(8,128)(2,1)} %param.9), kind=kOutput, calls=%fused_computation.4 | convolution fusion | flops 268435456 | bytes 2883584 | tf_op jit(solution)/shard_map/dot_general | solution.py:52
  6.9 3.4 %fusion.12 = f32[1024,128]{1,0:T(8,128)} fusion(f32[1024,128]{1,0:T(8,128)S(1)} %fusion.2, bf16[2,1024,1024]{2,1,0:T(8,128)(2,1)} %param.9, bf16[1024,128]{1,0:T(8,128)(2,1)S(1)} %copy-done.4, s32[128]{0:T(128)S(1)} %get-tuple-element.15, s32[128]{0:T(128)S(1)} %get-tuple-element.16, pred[128]{0:T(512)(128)(4,1)S(1)} %get-tuple-element.17, ...), kind=kOutput, calls=%fused_computation.14 | convolution fusion | flops 302383104 | bytes 3409152 | tf_op jit(solution)/shard_map/dot_general | solution.py:55
  10.3 7.7 %all-to-all-start = ((f32[8,128,128]{2,1,0:T(8,128)}), f32[8,128,128]{2,1,0:T(8,128)S(1)}, u32[]{:S(2)}, u32[]{:S(2)}) async-start(f32[8,128,128]{2,1,0:T(8,128)} %bitcast.8), calls=%async_computation | async-start | bytes 1048576 | tf_op jit(solution)/shard_map/all_to_all | solution.py:98
  18.0 0.1 iota_compare_fusion.2
  18.1 3.0 %fusion.79 = (bf16[1,1024,640]{2,1,0:T(8,128)(2,1)S(1)}, bf16[1,1024,640]{2,1,0:T(8,128)(2,1)}) fusion(bf16[2,1024,640]{2,1,0:T(8,128)(2,1)} %param.8), kind=kLoop, calls=%fused_computation.87 | loop fusion | bytes 5242880 | tf_op jit(solution)/shard_map/slice | solution.py:90
  21.2 1.2 %reshape.63 = bf16[24,16384]{1,0:T(8,128)(2,1)} reshape(bf16[3072,128]{1,0:T(8,128)(2,1)S(1)} %pad_maximum_fusion) | data formatting | bytes 1572864 | tf_op jit(solution)/shard_map/reshape | solution.py:76
  22.4 1.6 %convolution_convert_fusion = bf16[40,16384]{1,0:T(8,128)(2,1)S(1)} fusion(pred[40,24]{1,0:T(8,128)(4,1)S(1)} %eq.56, bf16[24,16384]{1,0:T(8,128)(2,1)} %reshape.63), kind=kOutput, calls=%fused_computation | convolution fusion | flops 32112640 | bytes 2098112 | tf_op jit(solution)/shard_map/dot_general | solution.py:85
  24.0 1.7 %reshape_reshape.3 = bf16[8,640,128]{2,1,0:T(8,128)(2,1)} reshape(bf16[40,16384]{1,0:T(8,128)(2,1)S(1)} %convolution_convert_fusion) | data formatting | bytes 2621440 | tf_op jit(solution)/shard_map/reshape;reshape | solution.py:88
  25.7 1.7 %reshape.64 = bf16[5120,128]{1,0:T(8,128)(2,1)} reshape(bf16[40,16384]{1,0:T(8,128)(2,1)S(1)} %convolution_convert_fusion) | data formatting | bytes 2621440 | tf_op jit(solution)/shard_map/reshape | solution.py:86
  27.4 2.0 %convolution_convert_fusion.1 = bf16[5120,128]{1,0:T(8,128)(2,1)S(1)} fusion(bf16[5120,128]{1,0:T(8,128)(2,1)} %reshape.64, s32[128]{0:T(128)S(1)} %get-tuple-element.15, s32[128]{0:T(128)S(1)} %get-tuple-element.16, pred[128]{0:T(512)(128)(4,1)S(1)} %get-tuple-element.17, pred[128]{0:T(512)(128)(4,1)S(1)} %get-tuple-element.18), kind=kOutput, calls=%fused_computation.1 | convolution fusion | flops 168558592 | bytes 2622720 | tf_op jit(solution)/shard_map/dot_general | solution.py:40
  29.4 0.1 copy-done.2
  29.5 1.3 %fusion.80 = f32[8,128,128]{1,2,0:T(8,128)} fusion(bf16[8,128,640]{2,1,0:T(8,128)(2,1)S(1)} %bitcast.87, bf16[8,640,128]{2,1,0:T(8,128)(2,1)S(1)} %copy-done.2), kind=kOutput, calls=%fused_computation.88 | convolution fusion | flops 167772160 | bytes 3145728 | tf_op jit(solution)/shard_map/ilm,imc->ilc/dot_general | solution.py:91
  30.8 2.6 %all-to-all-done = f32[8,128,128]{2,1,0:T(8,128)S(1)} async-done(((f32[8,128,128]{2,1,0:T(8,128)}), f32[8,128,128]{2,1,0:T(8,128)S(1)}, u32[]{:S(2)}, u32[]{:S(2)}) %all-to-all-start) | async-done | bytes 524320 | tf_op jit(solution)/shard_map/all_to_all | solution.py:98
  33.3 0.1 subtract_convert_fusion
  33.4 2.5 %fusion.30 = f32[128,512]{1,0:T(8,128)} fusion(bf16[1024,128]{1,0:T(8,128)(2,1)S(1)} %bitcast.94, bf16[2,512,1024]{2,1,0:T(8,128)(2,1)} %param.10), kind=kOutput, calls=%fused_computation.36 | convolution fusion | flops 134217728 | bytes 1572864 | tf_op jit(solution)/shard_map/dot_general | solution.py:45
  36.0 1.2 %fusion.32 = f32[128,512]{1,0:T(8,128)} fusion(bf16[1024,128]{1,0:T(8,128)(2,1)S(1)} %bitcast.93, bf16[2,512,1024]{2,1,0:T(8,128)(2,1)S(1)} %copy-done.5), kind=kOutput, calls=%fused_computation.38 | convolution fusion | flops 134217728 | bytes 1572864 | tf_op jit(solution)/shard_map/dot_general | solution.py:45
  37.2 0.8 %fusion.42 = (bf16[1024,128]{1,0:T(8,128)(2,1)S(1)}, bf16[1024,128]{1,0:T(8,128)(2,1)}) fusion(f32[8,128,128]{2,1,0:T(8,128)S(1)} %all-to-all-done), kind=kLoop, calls=%fused_computation.51 | loop fusion | flops 524288 | bytes 1048576 | tf_op jit(solution)/shard_map/convert_element_type | solution.py:62
  37.9 2.7 %fusion.21 = f32[128,512]{1,0:T(8,128)} fusion(f32[128,512]{1,0:T(8,128)} %fusion.30, bf16[1024,128]{1,0:T(8,128)(2,1)S(1)} %get-tuple-element.9, bf16[2,512,1024]{2,1,0:T(8,128)(2,1)} %param.10, s32[128]{0:T(128)S(1)} %get-tuple-element.15, s32[128]{0:T(128)S(1)} %get-tuple-element.16, pred[128]{0:T(512)(128)(4,1)S(1)} %get-tuple-element.17, ...), kind=kOutput, calls=%fused_computation.25 | convolution fusion | flops 168099840 | bytes 1836288 | tf_op jit(solution)/shard_map/dot_general | solution.py:46
  40.6 2.1 %fusion.19 = f32[16,4,8,128]{3,2,1,0:T(8,128)S(1)} fusion(f32[128,512]{1,0:T(8,128)} %fusion.21, f32[128,512]{1,0:T(8,128)} %fusion.32, bf16[1024,128]{1,0:T(8,128)(2,1)} %get-tuple-element.10, bf16[2,512,1024]{2,1,0:T(8,128)(2,1)} %param.10, s32[128]{0:T(128)S(1)} %get-tuple-element.15, s32[128]{0:T(128)S(1)} %get-tuple-element.16, ...), kind=kOutput, calls=%fused_computation.23 | convolution fusion | flops 168165376 | bytes 2098432 | tf_op jit(solution)/shard_map/dot_general | solution.py:46
  42.7 0.7 %copy.27 = f32[16,4,8,128]{3,2,0,1:T(8,128)} copy(f32[16,4,8,128]{3,2,1,0:T(8,128)S(1)} %fusion.19) | data formatting | bytes 524288 | tf_op jit(solution)/shard_map/reshape | solution.py:102
  43.5 3.4 %all-to-all-start.1 = ((f32[4,128,128]{1,2,0:T(8,128)}), f32[4,128,128]{1,2,0:T(8,128)S(1)}, u32[]{:S(2)}, u32[]{:S(2)}) async-start(f32[4,128,128]{1,2,0:T(8,128)} %bitcast.90), calls=%async_computation.1 | async-start | bytes 524288 | tf_op jit(solution)/shard_map/all_to_all | solution.py:103
  46.9 1.3 %convolution_add_fusion.2 = f32[8,128,128]{1,2,0:T(8,128)} fusion(f32[8,128,128]{1,2,0:T(8,128)S(1)} %copy-done.3, bf16[8,128,640]{2,1,0:T(8,128)(2,1)S(1)} %bitcast.86, bf16[8,640,128]{2,1,0:T(8,128)(2,1)S(1)} %bitcast.88), kind=kOutput, calls=%fused_computation.15 | convolution fusion | flops 167903232 | bytes 3670016 | tf_op jit(solution)/shard_map/ilm,imc->ilc/dot_general | solution.py:92
  48.2 1.4 %copy.22 = f32[1024,128]{0,1:T(8,128)S(1)} copy(f32[1024,128]{1,0:T(8,128)} %bitcast.89) | data formatting | bytes 1048576 | tf_op jit(solution)/shard_map/reshape | solution.py:95
  49.6 3.3 %all-to-all-done.1 = f32[4,128,128]{1,2,0:T(8,128)S(1)} async-done(((f32[4,128,128]{1,2,0:T(8,128)}), f32[4,128,128]{1,2,0:T(8,128)S(1)}, u32[]{:S(2)}, u32[]{:S(2)}) %all-to-all-start.1) | async-done | bytes 262176 | tf_op jit(solution)/shard_map/all_to_all | solution.py:103
  52.8 0.1 copy.19
  53.1 1.3 %fusion.24 = f32[128,1024]{1,0:T(8,128)} fusion(bf16[512,128]{1,0:T(8,128)(2,1)S(1)} %bitcast.92, bf16[2,1024,512]{2,1,0:T(8,128)(2,1)S(1)} %copy-done), kind=kOutput, calls=%fused_computation.30 | convolution fusion | flops 134217728 | bytes 1703936 | tf_op jit(solution)/shard_map/dot_general | solution.py:45
  54.4 1.3 %fusion.26 = f32[128,1024]{1,0:T(8,128)} fusion(bf16[512,128]{1,0:T(8,128)(2,1)S(1)} %bitcast.91, bf16[2,1024,512]{2,1,0:T(8,128)(2,1)S(1)} %copy-done), kind=kOutput, calls=%fused_computation.32 | convolution fusion | flops 134217728 | bytes 1703936 | tf_op jit(solution)/shard_map/dot_general | solution.py:45
  55.6 1.7 %convolution_add_fusion = f32[128,1024]{1,0:T(8,128)S(1)} fusion(f32[128,1024]{1,0:T(8,128)} %fusion.24, bf16[512,128]{1,0:T(8,128)(2,1)S(1)} %get-tuple-element.5, bf16[2,1024,512]{2,1,0:T(8,128)(2,1)S(1)} %copy-done, s32[128]{0:T(128)S(1)} %get-tuple-element.15, s32[128]{0:T(128)S(1)} %get-tuple-element.16, pred[128]{0:T(512)(128)(4,1)S(1)} %get-tuple-element.17, ...), kind=kOutput, calls=%fused_computation.8 | convolution fusion | flops 151322624 | bytes 2230272 | tf_op jit(solution)/shard_map/dot_general | solution.py:46
  57.3 1.7 %fusion.15 = bf16[1024,128]{0,1:T(8,128)(2,1)S(1)} fusion(f32[1024,128]{0,1:T(8,128)S(1)} %copy.22, f32[128,1024]{1,0:T(8,128)S(1)} %convolution_add_fusion, f32[128,1024]{1,0:T(8,128)} %fusion.26, bf16[512,128]{1,0:T(8,128)(2,1)S(1)} %get-tuple-element.6, bf16[2,1024,512]{2,1,0:T(8,128)(2,1)S(1)} %copy-done, s32[128]{0:T(128)S(1)} %get-tuple-element.15, ...), kind=kOutput, calls=%fused_computation.16 | convolution fusion | flops 151715840 | bytes 3016704 | tf_op jit(solution)/shard_map/dot_general | solution.py:46
  59.0 0.8 %copy.23 = bf16[1024,128]{1,0:T(8,128)(2,1)} copy(bf16[1024,128]{0,1:T(8,128)(2,1)S(1)} %fusion.15) | data formatting | bytes 524288 | tf_op jit(solution)/shard_map/convert_element_type | solution.py:107
  (22 shorter events, 0.2 us)
Async XLA Ops:
  0.0 6.8 %copy-start.4 = (bf16[1024,128]{1,0:T(8,128)(2,1)S(1)}, bf16[1024,128]{1,0:T(8,128)(2,1)}, u32[]{:S(2)}) copy-start(bf16[1024,128]{1,0:T(8,128)(2,1)} %param.6) | copy-start | bytes 786436
  0.0 21.1 %collective-permute-start.1 = (bf16[1024,128]{1,0:T(8,128)(2,1)}, bf16[1024,128]{1,0:T(8,128)(2,1)S(1)}, u32[]{:S(2)}, u32[]{:S(2)}) collective-permute-start(bf16[1024,128]{1,0:T(8,128)(2,1)} %param.6), channel_id=1, source_target_pairs={{1,0},{2,1},{3,2},{4,3},{5,4},{6,5},{7,6},{8,7},{9,8},{10,9},{11,1... | collective-permute-start | bytes 786440 | tf_op jit(solution)/shard_map/ppermute | solution.py:22
  1.4 19.7 %collective-permute-start = (bf16[1024,128]{1,0:T(8,128)(2,1)}, bf16[1024,128]{1,0:T(8,128)(2,1)S(1)}, u32[]{:S(2)}, u32[]{:S(2)}) collective-permute-start(bf16[1024,128]{1,0:T(8,128)(2,1)} %param.6), channel_id=1, source_target_pairs={{0,1},{1,2},{2,3},{3,4},{4,5},{5,6},{6,7},{7,8},{8,9},{9,10},{10,1... | collective-permute-start | bytes 786440 | tf_op jit(solution)/shard_map/ppermute | solution.py:20
  6.8 11.1 %copy-start.6 = (s32[8,5]{1,0:T(8,128)S(1)}, s32[8,5]{1,0:T(8,128)}, u32[]{:S(2)}) copy-start(s32[8,5]{1,0:T(8,128)} %param.7) | copy-start | bytes 484
  10.3 23.1 %all-to-all-start = ((f32[8,128,128]{2,1,0:T(8,128)}), f32[8,128,128]{2,1,0:T(8,128)S(1)}, u32[]{:S(2)}, u32[]{:S(2)}) async-start(f32[8,128,128]{2,1,0:T(8,128)} %bitcast.8), calls=%async_computation | async-start | bytes 1048576 | tf_op jit(solution)/shard_map/all_to_all | solution.py:98
  27.4 2.0 %copy-start.1 = (bf16[1,1024,640]{2,1,0:T(8,128)(2,1)S(1)}, bf16[1,1024,640]{2,1,0:T(8,128)(2,1)}, u32[]{:S(2)}) copy-start(bf16[1,1024,640]{2,1,0:T(8,128)(2,1)} %get-tuple-element.14) | copy-start | bytes 3932164
  27.4 2.1 %copy-start.2 = (bf16[8,640,128]{2,1,0:T(8,128)(2,1)S(1)}, bf16[8,640,128]{2,1,0:T(8,128)(2,1)}, u32[]{:S(2)}) copy-start(bf16[8,640,128]{2,1,0:T(8,128)(2,1)} %reshape_reshape.3) | copy-start | bytes 3932164
  33.3 2.7 %copy-start.5 = (bf16[2,512,1024]{2,1,0:T(8,128)(2,1)S(1)}, bf16[2,512,1024]{2,1,0:T(8,128)(2,1)}, u32[]{:S(2)}) copy-start(bf16[2,512,1024]{2,1,0:T(8,128)(2,1)} %param.10) | copy-start | bytes 6291460
  37.9 8.9 %copy-start.3 = (f32[8,128,128]{1,2,0:T(8,128)S(1)}, f32[8,128,128]{1,2,0:T(8,128)}, u32[]{:S(2)}) copy-start(f32[8,128,128]{1,2,0:T(8,128)} %fusion.80) | copy-start | bytes 1572868
  43.5 9.4 %all-to-all-start.1 = ((f32[4,128,128]{1,2,0:T(8,128)}), f32[4,128,128]{1,2,0:T(8,128)S(1)}, u32[]{:S(2)}, u32[]{:S(2)}) async-start(f32[4,128,128]{1,2,0:T(8,128)} %bitcast.90), calls=%async_computation.1 | async-start | bytes 524288 | tf_op jit(solution)/shard_map/all_to_all | solution.py:103
  48.2 4.9 %copy-start = (bf16[2,1024,512]{2,1,0:T(8,128)(2,1)S(1)}, bf16[2,1024,512]{2,1,0:T(8,128)(2,1)}, u32[]{:S(2)}) copy-start(bf16[2,1024,512]{2,1,0:T(8,128)(2,1)} %param.11) | copy-start | bytes 6291460
where the time goes:
time: 60.5 us; the launch traced here: 59.9 us
  matrix products  26.4 us (44%)
  starting transfers between devices  15.6 us (26%)
  local copies, waits for them, and re-layouts  10.8 us (18%)
  waiting for transfers between devices  5.83 us (10%)
  other arithmetic  1.08 us (2%)
    dot_general x4, matrix products, multiply_flat(): jnp.dot(imag_part, turned, preferred_element_type=jnp.float32)  8.17 us
    all_to_all x1, starting transfers between devices, on_device(): lax.all_to_all(shaped, 'row', split_axis=0, concat_axis=0, tiled=True)  7.7 us
    dot_general x4, matrix products, multiply_flat(): summed = jnp.dot(real_part, flat_data, preferred_element_type=jnp.float32)  6.28 us
    all_to_all x1, starting transfers between devices, on_device(): lax.all_to_all(middle, 'col', split_axis=0, concat_axis=0, tiled=True)  3.41 us
    dot_general x1, matrix products, project_flat(): lax.dot_general(imag_part, turned, contract_dims, preferred_element_type=...  3.4 us
    all_to_all x1, waiting for transfers between devices, on_device(): lax.all_to_all(middle, 'col', split_axis=0, concat_axis=0, tiled=True)  3.26 us
    ppermute x1, starting transfers between devices, with_halo(): lax.ppermute(tail, axis, [(i, (i + 1) % count) for i in range(ends)])  3.05 us
    slice x1, local copies, waits for them, and re-layouts, on_device(): blocks_im = near_blocks[1].reshape(leaves_here, LEAF, NEAR * LEAF)  3.03 us
  transfers between devices with their start and end apart: 4, of which 2 were waited for; matrix products, arithmetic and copies ran while one was open for 35% of the time, Pallas kernels for 0%

commit v1 on v0

v1 whole, which is shorter than its diff:
```python
import functools

import jax
import jax.numpy as jnp
from jax import lax
from jax.experimental import pallas as pl
from jax.experimental.pallas import tpu as pltpu
from jax.sharding import PartitionSpec as P

RANK = 128
LEAF = 128
REACH = 8
NEAR = 5
MIB = 1 << 20
VMEM = pl.BlockSpec(memory_space=pltpu.VMEM)
SMEM = pl.BlockSpec(memory_space=pltpu.SMEM)
NT = (((1,), (1,)), ((), ()))


def params(mib):
    return pltpu.CompilerParams(vmem_limit_bytes=mib * MIB)


def cost(flops, moved):
    return pl.CostEstimate(flops=flops, bytes_accessed=moved, transcendentals=0)


def dot(a, b):
    return jnp.dot(a, b, preferred_element_type=jnp.float32)


def turn_rows(v):
    half = v.shape[0] // 2
    return jnp.concatenate([-v[half:], v[:half]], axis=0)


def turn_lanes(v):
    half = v.shape[-1] // 2
    rolled = pltpu.roll(v, half, v.ndim - 1)
    lane = lax.broadcasted_iota(jnp.int32, v.shape, v.ndim - 1)
    return jnp.where(lane < half, -rolled, rolled)


def project_kernel(x_ref, v_ref, o_ref, lhs):
    count = x_ref.shape[0]
    turned = x_ref[...].astype(jnp.float32).T.astype(jnp.bfloat16)
    lhs[:, :count] = turned
    lhs[:, count:] = turn_rows(turned)
    groups = o_ref.shape[0]
    step = 2
    for g in range(0, groups, step):
        lanes = slice(g * RANK, (g + step) * RANK)
        total = dot(lhs[:, :count], v_ref[0, :, lanes]) + dot(lhs[:, count:], v_ref[1, :, lanes])
        for s in range(step):
            o_ref[g + s] = total[:, s * RANK : (s + 1) * RANK].astype(jnp.bfloat16)


def project(x, v):
    groups = v.shape[2] // RANK
    count, width = x.shape
    return pl.pallas_call(
        project_kernel,
        out_shape=jax.ShapeDtypeStruct((groups, width, RANK), jnp.bfloat16),
        in_specs=[VMEM, VMEM],
        out_specs=VMEM,
        scratch_shapes=[pltpu.VMEM((width, 2 * count), jnp.bfloat16)],
        compiler_params=params(12),
        cost_estimate=cost(4 * width * v.shape[1] * v.shape[2], v.size * 2),
        name="project",
    )(x, v)


def near_kernel(list_ref, own_ref, first_ref, second_ref, p_ref, o_ref, table, rhs):
    leaves = own_ref.shape[0] // LEAF
    width = own_ref.shape[1]
    here = lax.axis_index(("row", "col"))
    odd = lax.rem(here, 2)
    base = here * leaves
    table[pl.ds(0, leaves)] = own_ref[...].reshape(leaves, LEAF, width)
    table[pl.ds(leaves, leaves)] = first_ref[...].reshape(leaves, LEAF, width)
    table[pl.ds(2 * leaves, leaves)] = second_ref[...].reshape(leaves, LEAF, width)
    for i in range(leaves):
        rows = slice(i * LEAF, (i + 1) * LEAF)
        for j in range(NEAR):
            at = list_ref[i, j] - base
            left = at < 0
            right = at >= leaves
            below = at + leaves * jnp.where(odd == 1, 2, 3)
            above = at + leaves * jnp.where(odd == 1, 1, 0)
            slot = jnp.where(left, below, jnp.where(right, above, at))
            rhs[i % 2, j * LEAF : (j + 1) * LEAF] = table[slot]
        data = rhs[i % 2]
        straight = dot(p_ref[0, rows], data)
        crossed = dot(p_ref[1, rows], data)
        o_ref[rows] = straight + turn_lanes(crossed)


def near(near_list, own, first, second, blocks):
    count, width = own.shape
    leaves = count // LEAF
    return pl.pallas_call(
        near_kernel,
        out_shape=jax.ShapeDtypeStruct((count, width), jnp.float32),
        in_specs=[SMEM, VMEM, VMEM, VMEM, VMEM],
        out_specs=VMEM,
        scratch_shapes=[
            pltpu.VMEM((3 * leaves, LEAF, width), jnp.bfloat16),
            pltpu.VMEM((2, NEAR * LEAF, width), jnp.bfloat16),
        ],
        compiler_params=params(8),
        cost_estimate=cost(4 * width * blocks.shape[1] * blocks.shape[2], blocks.size * 2),
        name="near",
    )(near_list, own, first, second, blocks)


def mid_kernel(a_ref, c_ref, o_ref, rhs):
    groups, width = a_ref.shape[0], a_ref.shape[1]
    for r in range(groups):
        lanes = slice(r * RANK, (r + 1) * RANK)
        rhs[0, :, lanes] = a_ref[r]
        rhs[1, :, lanes] = turn_rows(a_ref[r])
    for k in range(o_ref.shape[0]):
        at = lax.axis_index("col") ^ k
        rows = pl.ds(pl.multiple_of(at * RANK, RANK), RANK)
        total = lax.dot_general(c_ref[0, rows], rhs[0], NT, preferred_element_type=jnp.float32)
        total += lax.dot_general(c_ref[1, rows], rhs[1], NT, preferred_element_type=jnp.float32)
        o_ref[k] = total.astype(jnp.bfloat16)


def mid(arrived, coupling):
    groups, width, _ = arrived.shape
    blocks = coupling.shape[1] // RANK
    return pl.pallas_call(
        mid_kernel,
        out_shape=jax.ShapeDtypeStruct((blocks, RANK, width), jnp.bfloat16),
        in_specs=[VMEM, VMEM],
        out_specs=VMEM,
        scratch_shapes=[pltpu.VMEM((2, width, groups * RANK), jnp.bfloat16)],
        compiler_params=params(8),
        cost_estimate=cost(4 * width * coupling.shape[1] * coupling.shape[2], coupling.size * 2),
        name="mid",
    )(arrived, coupling)


def far_kernel(*refs):
    *landed, u_ref, n_ref, o_ref, data, crossed = refs
    blocks = len(landed)
    for k in range(blocks):
        at = lax.axis_index("col") ^ k
        rows = pl.ds(pl.multiple_of(at * RANK, RANK), RANK)
        value = landed[k][...]
        data[rows] = value
        crossed[rows] = turn_lanes(value.astype(jnp.float32)).astype(jnp.bfloat16)
    step = 256
    for i in range(0, o_ref.shape[0], step):
        rows = slice(i, i + step)
        total = dot(u_ref[0, rows], data[...]) + dot(u_ref[1, rows], crossed[...])
        o_ref[rows] = (total + n_ref[rows]).astype(jnp.bfloat16)


def far(landed, factors, near_field):
    count, width = near_field.shape
    ranks = len(landed) * RANK
    return pl.pallas_call(
        far_kernel,
        out_shape=jax.ShapeDtypeStruct((count, width), jnp.bfloat16),
        in_specs=[VMEM] * (len(landed) + 2),
        out_specs=VMEM,
        scratch_shapes=[pltpu.VMEM((ranks, width), jnp.bfloat16)] * 2,
        compiler_params=params(8),
        cost_estimate=cost(4 * width * factors.shape[1] * factors.shape[2], factors.size * 2),
        name="far",
    )(*landed, factors, near_field)


def on_device(excitation, near_list, near_blocks, col_factors, coupling, row_factors):
    row_count = lax.axis_size("row")
    col_count = lax.axis_size("col")
    total = row_count * col_count
    axes = ("row", "col")
    inner = [(i, i ^ 1) for i in range(total)]
    outer = [(i, ((i + 1) ^ 1) - 1) for i in range(1, total - 1)]
    second = lax.ppermute(excitation, axes, outer)
    first = lax.ppermute(excitation, axes, inner)
    compressed = project(excitation, col_factors)
    arrived = lax.all_to_all(compressed, "row", split_axis=0, concat_axis=0, tiled=True)
    near_field = near(near_list, excitation, first, second, near_blocks)
    middle = mid(arrived, coupling)
    landed = [middle[0]]
    for k in range(1, col_count):
        landed.append(lax.ppermute(middle[k], "col", [(i, i ^ k) for i in range(col_count)]))
    return far(landed, row_factors, near_field)


def solution(mesh):
    return jax.shard_map(
        on_device,
        mesh=mesh,
        in_specs=(
            P(("row", "col"), None),
            P(("row", "col"), None),
            P(None, ("row", "col"), None),
            P(None, ("row", "col"), None),
            P(None, ("row", "col"), None),
            P(None, ("row", "col"), None),
        ),
        out_specs=P(("row", "col"), None),
        check_vma=False,
    )
```

time: 60.5 us -> 29.5 us (0.49)
  matrix products: 26.4 us -> 0 us
  local copies, waits for them, and re-layouts: 10.8 us -> 4.76 us
  Pallas kernels: 0 us -> 5.65 us
  starting transfers between devices: 15.6 us -> 10.9 us
  waiting for transfers between devices: 5.83 us -> 7.77 us
  other arithmetic: 1.08 us -> 0 us
    dot_general x14 -> x0, matrix products: 26.4 us -> none  [the longest x4 8.17 us: multiply_flat(): jnp.dot(imag_part, turned, preferred_element_type=jnp.float32)]
    pallas_call x0 -> x4, Pallas kernels: none -> 5.65 us  [the longest x1 1.91 us: near(): pl.pallas_call(near_kernel, out_shape=jax.ShapeDtypeStruct((count, width)...]
    reshape x4 -> x0, local copies, waits for them, and re-layouts: 5.01 us -> none  [the longest x1 1.66 us: on_device(): pieces = pieces.reshape(leaves_here * NEAR * LEAF, width_cols)]
    unnamed x14, local copies, waits for them, and re-layouts: 0.14 us -> 4.75 us
    all_to_all x2 -> x1, starting transfers between devices: 11.1 us -> 7.54 us  [on_device(): lax.all_to_all(compressed, 'row', split_axis=0, concat_axis=0, tiled=True)]
    slice x1 -> x0, local copies, waits for them, and re-layouts: 3.03 us -> none  [on_device(): blocks_im = near_blocks[1].reshape(leaves_here, LEAF, NEAR * LEAF)]
    all_to_all x2 -> x1, waiting for transfers between devices: 5.82 us -> 7.56 us  [on_device(): lax.all_to_all(compressed, 'row', split_axis=0, concat_axis=0, tiled=True)]
    another operation x1 -> x0, local copies, waits for them, and re-layouts: 1.66 us -> none  [on_device(): pieces = pieces.reshape(leaves_here, NEAR * LEAF, width_cols)]
  transfers between devices with their start and end apart: 4 -> 6, of which waited for: 2 -> 2; matrix products, arithmetic and copies ran while one was open for 35% -> 0% of each run, Pallas kernels for 0% -> 9%
where the time goes in v1:
time: 29.5 us; the launch traced here: 29.2 us
  starting transfers between devices  10.9 us (37%)
  waiting for transfers between devices  7.77 us (26%)
  Pallas kernels  5.65 us (19%)
  local copies, waits for them, and re-layouts  4.76 us (16%)
    all_to_all x1, waiting for transfers between devices, on_device(): lax.all_to_all(compressed, 'row', split_axis=0, concat_axis=0, tiled=True)  7.56 us
    all_to_all x1, starting transfers between devices, on_device(): lax.all_to_all(compressed, 'row', split_axis=0, concat_axis=0, tiled=True)  7.54 us
    unnamed x14, local copies, waits for them, and re-layouts  4.75 us
    ppermute x3, starting transfers between devices, on_device(): lax.ppermute(middle[k], 'col', [(i, i ^ k) for i in range(col_count)])  1.92 us
    pallas_call x1, Pallas kernels, near(): pl.pallas_call(near_kernel, out_shape=jax.ShapeDtypeStruct((count, width)...  1.91 us
    pallas_call x1, Pallas kernels, far(): pl.pallas_call(far_kernel, out_shape=jax.ShapeDtypeStruct((count, width),...  1.52 us
    pallas_call x1, Pallas kernels, project(): pl.pallas_call(project_kernel, out_shape=jax.ShapeDtypeStruct((groups, wi...  1.5 us
    ppermute x1, starting transfers between devices, on_device(): second = lax.ppermute(excitation, axes, outer)  1.37 us
  transfers between devices with their start and end apart: 6, of which 2 were waited for; matrix products, arithmetic and copies ran while one was open for 0% of the time, Pallas kernels for 9%

profile of v1, /device:TPU:0, one launch (start us, length us, event | category | flops | bytes accessed | tf_op | source)
XLA Modules:
  0.0 29.2 jit_solution(9773796346861324787)
XLA Ops:
  0.0 0.0 copy-start
  0.0 2.2 %copy-done = bf16[2,1024,1024]{2,1,0:T(8,128)(2,1)S(1)} copy-done((bf16[2,1024,1024]{2,1,0:T(8,128)(2,1)S(1)}, bf16[2,1024,1024]{2,1,0:T(8,128)(2,1)}, u32[]{:S(2)}) %copy-start) | copy-done | bytes 4194328
  2.2 0.0 copy-start.4
  2.2 0.9 %copy-done.4 = bf16[1024,128]{1,0:T(8,128)(2,1)S(1)} copy-done((bf16[1024,128]{1,0:T(8,128)(2,1)S(1)}, bf16[1024,128]{1,0:T(8,128)(2,1)}, u32[]{:S(2)}) %copy-start.4) | copy-done | bytes 262168
  3.1 0.0 copy-start.5
  3.1 0.0 copy-start.6
  3.1 1.5 %project.1 = bf16[8,128,128]{2,1,0:T(8,128)(2,1)} custom-call(bf16[1024,128]{1,0:T(8,128)(2,1)S(1)} %copy-done.4, bf16[2,1024,1024]{2,1,0:T(8,128)(2,1)S(1)} %copy-done), custom_call_target="tpu_custom_call" | custom-call | flops 536870912 | bytes 4194304 | tf_op jit(solution)/shard_map/project/pallas_call | solution.py:61
  4.6 0.0 copy-start.1
  4.6 7.5 %all-to-all-start = ((bf16[8,128,128]{2,1,0:T(8,128)(2,1)}), bf16[8,128,128]{2,1,0:T(8,128)(2,1)S(1)}, u32[]{:S(2)}, u32[]{:S(2)}) async-start(bf16[8,128,128]{2,1,0:T(8,128)(2,1)} %project.1), calls=%async_computation | async-start | bytes 524288 | tf_op jit(solution)/shard_map/all_to_all | solution.py:186
  12.2 0.0 copy-done.5
  12.2 0.1 collective-permute-start.3
  12.3 1.4 %collective-permute-start.4 = (bf16[1024,128]{1,0:T(8,128)(2,1)S(1)}, bf16[1024,128]{1,0:T(8,128)(2,1)}, u32[]{:S(2)}, u32[]{:S(2)}) collective-permute-start(bf16[1024,128]{1,0:T(8,128)(2,1)S(1)} %copy-done.5), channel_id=1, source_target_pairs={{1,2},{2,1},{3,4},{4,3},{5,6},{6,5},{7,8},{8,7},{9,10},{10,9},{11,... | collective-permute-start | bytes 786440 | tf_op jit(solution)/shard_map/ppermute | solution.py:183
  13.6 7.6 %all-to-all-done.a_ref = bf16[8,128,128]{2,1,0:T(8,128)(2,1)S(1)} async-done(((bf16[8,128,128]{2,1,0:T(8,128)(2,1)}), bf16[8,128,128]{2,1,0:T(8,128)(2,1)S(1)}, u32[]{:S(2)}, u32[]{:S(2)}) %all-to-all-start) | async-done | bytes 262176 | tf_op jit(solution)/shard_map/all_to_all | solution.py:186
  21.2 0.0 copy-start.2
  21.2 1.6 %copy-done.2 = bf16[2,512,1024]{2,1,0:T(8,128)(2,1)S(1)} copy-done((bf16[2,512,1024]{2,1,0:T(8,128)(2,1)S(1)}, bf16[2,512,1024]{2,1,0:T(8,128)(2,1)}, u32[]{:S(2)}) %copy-start.2) | copy-done | bytes 2097176
  22.8 0.7 %mid.1 = bf16[4,128,128]{2,1,0:T(8,128)(2,1)S(1)} custom-call(bf16[8,128,128]{2,1,0:T(8,128)(2,1)S(1)} %all-to-all-done.a_ref, bf16[2,512,1024]{2,1,0:T(8,128)(2,1)S(1)} %copy-done.2), custom_call_target="tpu_custom_call" | custom-call | flops 268435456 | bytes 2097152 | tf_op jit(solution)/shard_map/mid/pallas_call | solution.py:133
  23.5 0.0 copy-start.3
  23.6 0.1 collective-permute-start.2
  23.6 1.5 %collective-permute-start.1 = (bf16[128,128]{1,0:T(8,128)(2,1)S(1)}, bf16[128,128]{1,0:T(8,128)(2,1)S(1)}, u32[]{:S(2)}, u32[]{:S(2)}) collective-permute-start(bf16[128,128]{1,0:T(8,128)(2,1)S(1)} %get-tuple-element.6), channel_id=1, source_target_pairs={{0,2},{1,3},{2,0},{3,1},{4,6},{5,7},{6,4},{7,5},{8,10},{9,11},{10,... | collective-permute-start | bytes 98312 | tf_op jit(solution)/shard_map/ppermute | solution.py:191
  25.1 0.4 %collective-permute-start = (bf16[128,128]{1,0:T(8,128)(2,1)S(1)}, bf16[128,128]{1,0:T(8,128)(2,1)S(1)}, u32[]{:S(2)}, u32[]{:S(2)}) collective-permute-start(bf16[128,128]{1,0:T(8,128)(2,1)S(1)} %get-tuple-element.7), channel_id=1, source_target_pairs={{0,1},{1,0},{2,3},{3,2},{4,5},{5,4},{6,7},{7,6},{8,9},{9,8},{10,11... | collective-permute-start | bytes 98312 | tf_op jit(solution)/shard_map/ppermute | solution.py:191
  25.5 0.0 collective-permute-done.3.first_ref
  25.5 0.0 collective-permute-done.4.second_ref
  25.5 0.0 copy-done.6
  25.5 0.0 copy-done.1
  25.5 1.9 %near.1.refs_5_ = f32[1024,128]{1,0:T(8,128)S(1)} custom-call(s32[8,5]{1,0:T(8,128)S(1)} %copy-done.6, bf16[1024,128]{1,0:T(8,128)(2,1)S(1)} %copy-done.5, bf16[1024,128]{1,0:T(8,128)(2,1)S(1)} %collective-permute-done.3.first_ref, bf16[1024,128]{1,0:T(8,128)(2,1)} %collective-permute-done.4.second_ref, bf16[2,1024,640]{2,1,0:T(8,128)(2,1)S(1)} %copy-done.1), custom_call_target="tpu_custom_call" | custom-call | flops 335544320 | bytes 2621440 | tf_op jit(solution)/shard_map/near/pallas_call | solution.py:101
  27.4 0.0 collective-permute-done.2.refs_3_
  27.4 0.2 collective-permute-done.1.refs_2_
  27.6 0.0 collective-permute-done.refs_1_
  27.6 0.0 copy-done.3
  27.6 1.5 %far.1 = bf16[1024,128]{1,0:T(8,128)(2,1)} custom-call(bf16[128,128]{1,0:T(8,128)(2,1)S(1)} %get-tuple-element.8.refs_0_, bf16[128,128]{1,0:T(8,128)(2,1)S(1)} %collective-permute-done.refs_1_, bf16[128,128]{1,0:T(8,128)(2,1)S(1)} %collective-permute-done.1.refs_2_, bf16[128,128]{1,0:T(8,128)(2,1)S(1)} %collective-permute-done.2.refs_3_, ...), custom_call_target="tpu_custom_call" | custom-call | flops 268435456 | bytes 2097152 | tf_op jit(solution)/shard_map/far/pallas_call | solution.py:164
  (1 shorter events, 0.0 us)
Async XLA Ops:
  0.0 2.2 %copy-start = (bf16[2,1024,1024]{2,1,0:T(8,128)(2,1)S(1)}, bf16[2,1024,1024]{2,1,0:T(8,128)(2,1)}, u32[]{:S(2)}) copy-start(bf16[2,1024,1024]{2,1,0:T(8,128)(2,1)} %v_ref.1) | copy-start | bytes 12582916
  2.2 0.9 %copy-start.4 = (bf16[1024,128]{1,0:T(8,128)(2,1)S(1)}, bf16[1024,128]{1,0:T(8,128)(2,1)}, u32[]{:S(2)}) copy-start(bf16[1024,128]{1,0:T(8,128)(2,1)} %own_ref.1) | copy-start | bytes 786436
  3.1 9.0 %copy-start.5 = (bf16[1024,128]{1,0:T(8,128)(2,1)S(1)}, bf16[1024,128]{1,0:T(8,128)(2,1)}, u32[]{:S(2)}) copy-start(bf16[1024,128]{1,0:T(8,128)(2,1)} %own_ref.1) | copy-start | bytes 786436
  3.1 22.4 %copy-start.6 = (s32[8,5]{1,0:T(8,128)S(1)}, s32[8,5]{1,0:T(8,128)}, u32[]{:S(2)}) copy-start(s32[8,5]{1,0:T(8,128)} %list_ref.1) | copy-start | bytes 484
  4.6 20.9 %copy-start.1 = (bf16[2,1024,640]{2,1,0:T(8,128)(2,1)S(1)}, bf16[2,1024,640]{2,1,0:T(8,128)(2,1)}, u32[]{:S(2)}) copy-start(bf16[2,1024,640]{2,1,0:T(8,128)(2,1)} %p_ref.1) | copy-start | bytes 7864324
  4.6 16.6 %all-to-all-start = ((bf16[8,128,128]{2,1,0:T(8,128)(2,1)}), bf16[8,128,128]{2,1,0:T(8,128)(2,1)S(1)}, u32[]{:S(2)}, u32[]{:S(2)}) async-start(bf16[8,128,128]{2,1,0:T(8,128)(2,1)} %project.1), calls=%async_computation | async-start | bytes 524288 | tf_op jit(solution)/shard_map/all_to_all | solution.py:186
  12.2 13.3 %collective-permute-start.3 = (bf16[1024,128]{1,0:T(8,128)(2,1)S(1)}, bf16[1024,128]{1,0:T(8,128)(2,1)S(1)}, u32[]{:S(2)}, u32[]{:S(2)}) collective-permute-start(bf16[1024,128]{1,0:T(8,128)(2,1)S(1)} %copy-done.5), channel_id=1, source_target_pairs={{0,1},{1,0},{2,3},{3,2},{4,5},{5,4},{6,7},{7,6},{8,9},{9,8},{10,11... | collective-permute-start | bytes 786440 | tf_op jit(solution)/shard_map/ppermute | solution.py:184
  12.3 13.2 %collective-permute-start.4 = (bf16[1024,128]{1,0:T(8,128)(2,1)S(1)}, bf16[1024,128]{1,0:T(8,128)(2,1)}, u32[]{:S(2)}, u32[]{:S(2)}) collective-permute-start(bf16[1024,128]{1,0:T(8,128)(2,1)S(1)} %copy-done.5), channel_id=1, source_target_pairs={{1,2},{2,1},{3,4},{4,3},{5,6},{6,5},{7,8},{8,7},{9,10},{10,9},{11,... | collective-permute-start | bytes 786440 | tf_op jit(solution)/shard_map/ppermute | solution.py:183
  21.2 1.6 %copy-start.2 = (bf16[2,512,1024]{2,1,0:T(8,128)(2,1)S(1)}, bf16[2,512,1024]{2,1,0:T(8,128)(2,1)}, u32[]{:S(2)}) copy-start(bf16[2,512,1024]{2,1,0:T(8,128)(2,1)} %c_ref.1) | copy-start | bytes 6291460
  23.5 4.1 %copy-start.3 = (bf16[2,1024,512]{2,1,0:T(8,128)(2,1)S(1)}, bf16[2,1024,512]{2,1,0:T(8,128)(2,1)}, u32[]{:S(2)}) copy-start(bf16[2,1024,512]{2,1,0:T(8,128)(2,1)} %refs_4_.1) | copy-start | bytes 6291460
  23.6 3.9 %collective-permute-start.2 = (bf16[128,128]{1,0:T(8,128)(2,1)S(1)}, bf16[128,128]{1,0:T(8,128)(2,1)S(1)}, u32[]{:S(2)}, u32[]{:S(2)}) collective-permute-start(bf16[128,128]{1,0:T(8,128)(2,1)S(1)} %get-tuple-element.5), channel_id=1, source_target_pairs={{0,3},{1,2},{2,1},{3,0},{4,7},{5,6},{6,5},{7,4},{8,11},{9,10},{10,... | collective-permute-start | bytes 98312 | tf_op jit(solution)/shard_map/ppermute | solution.py:191
  23.6 4.0 %collective-permute-start.1 = (bf16[128,128]{1,0:T(8,128)(2,1)S(1)}, bf16[128,128]{1,0:T(8,128)(2,1)S(1)}, u32[]{:S(2)}, u32[]{:S(2)}) collective-permute-start(bf16[128,128]{1,0:T(8,128)(2,1)S(1)} %get-tuple-element.6), channel_id=1, source_target_pairs={{0,2},{1,3},{2,0},{3,1},{4,6},{5,7},{6,4},{7,5},{8,10},{9,11},{10,... | collective-permute-start | bytes 98312 | tf_op jit(solution)/shard_map/ppermute | solution.py:191
  25.1 2.5 %collective-permute-start = (bf16[128,128]{1,0:T(8,128)(2,1)S(1)}, bf16[128,128]{1,0:T(8,128)(2,1)S(1)}, u32[]{:S(2)}, u32[]{:S(2)}) collective-permute-start(bf16[128,128]{1,0:T(8,128)(2,1)S(1)} %get-tuple-element.7), channel_id=1, source_target_pairs={{0,1},{1,0},{2,3},{3,2},{4,5},{5,4},{6,7},{7,6},{8,9},{9,8},{10,11... | collective-permute-start | bytes 98312 | tf_op jit(solution)/shard_map/ppermute | solution.py:191

commit v2 on v1

v2 whole, which is shorter than its diff:
```python
import functools

import jax
import jax.numpy as jnp
from jax import lax
from jax.experimental import pallas as pl
from jax.experimental.pallas import tpu as pltpu
from jax.sharding import PartitionSpec as P

RANK = 128
LEAF = 128
NEAR = 5
MIB = 1 << 20
VMEM = pl.BlockSpec(memory_space=pltpu.VMEM)
HBM = pl.BlockSpec(memory_space=pltpu.HBM)
SMEM = pl.BlockSpec(memory_space=pltpu.SMEM)
NT = (((1,), (1,)), ((), ()))


def params(mib):
    return pltpu.CompilerParams(vmem_limit_bytes=mib * MIB)


def cost(flops, moved):
    return pl.CostEstimate(flops=flops, bytes_accessed=moved, transcendentals=0)


def dot(a, b):
    return jnp.dot(a, b, preferred_element_type=jnp.float32)


def turn_rows(v):
    half = v.shape[0] // 2
    return jnp.concatenate([-v[half:], v[:half]], axis=0)


def turn_lanes(v):
    half = v.shape[-1] // 2
    rolled = pltpu.roll(v, half, v.ndim - 1)
    lane = lax.broadcasted_iota(jnp.int32, v.shape, v.ndim - 1)
    return jnp.where(lane < half, -rolled, rolled)


def project_kernel(x_hbm, v_hbm, o_hbm, x_ref, v_ref, lhs, part, o_ref, x_sem, v_sem, o_sem):
    half = x_ref.shape[0] // 2
    wide = 2 * RANK
    pieces = v_ref.shape[2] // wide

    def fetch(k, p):
        rows = pl.ds(k * half, half)
        return pltpu.make_async_copy(v_hbm.at[p, rows], v_ref.at[p, rows], v_sem.at[k, p])

    def leave(n):
        rows = pl.ds(n * 2, 2)
        return pltpu.make_async_copy(o_ref.at[rows], o_hbm.at[rows], o_sem.at[n])

    def product(k, n):
        rows = slice(k * half, (k + 1) * half)
        lanes = slice(n * wide, (n + 1) * wide)
        return dot(lhs[0, :, rows], v_ref[0, rows, lanes]) + dot(lhs[1, :, rows], v_ref[1, rows, lanes])

    load = pltpu.make_async_copy(x_hbm, x_ref, x_sem)
    load.start()
    for k in range(2):
        for p in range(2):
            fetch(k, p).start()
    load.wait()
    turned = x_ref[...].astype(jnp.float32).T.astype(jnp.bfloat16)
    lhs[0] = turned
    lhs[1] = turn_rows(turned)
    for p in range(2):
        fetch(0, p).wait()
    for n in range(pieces):
        part[n] = product(0, n)
    for p in range(2):
        fetch(1, p).wait()
    for n in range(pieces):
        total = part[n] + product(1, n)
        for s in range(2):
            o_ref[n * 2 + s] = total[:, s * RANK : (s + 1) * RANK].astype(jnp.bfloat16)
        leave(n).start()
    for n in range(pieces):
        leave(n).wait()


def project(x, v):
    groups = v.shape[2] // RANK
    count, width = x.shape
    return pl.pallas_call(
        project_kernel,
        out_shape=jax.ShapeDtypeStruct((groups, width, RANK), jnp.bfloat16),
        in_specs=[HBM, HBM],
        out_specs=HBM,
        scratch_shapes=[
            pltpu.VMEM(x.shape, x.dtype),
            pltpu.VMEM(v.shape, v.dtype),
            pltpu.VMEM((2, width, count), v.dtype),
            pltpu.VMEM((groups // 2, width, 2 * RANK), jnp.float32),
            pltpu.VMEM((groups, width, RANK), v.dtype),
            pltpu.SemaphoreType.DMA(()),
            pltpu.SemaphoreType.DMA((2, 2)),
            pltpu.SemaphoreType.DMA((groups // 2,)),
        ],
        compiler_params=params(60),
        cost_estimate=cost(4 * width * v.shape[1] * v.shape[2], v.size * 2),
        name="project",
    )(x, v)


def slots_kernel(list_ref, o_ref):
    leaves = list_ref.shape[0]
    here = lax.axis_index(("row", "col"))
    odd = lax.rem(here, 2)
    at = list_ref[...] - here * leaves
    below = at + leaves * jnp.where(odd == 1, 2, 3)
    above = at + leaves * jnp.where(odd == 1, 1, 0)
    o_ref[...] = jnp.where(at < 0, below, jnp.where(at >= leaves, above, at))


def slots_of(near_list):
    return pl.pallas_call(
        slots_kernel,
        out_shape=jax.ShapeDtypeStruct(near_list.shape, jnp.int32),
        in_specs=[VMEM],
        out_specs=VMEM,
        compiler_params=params(1),
        cost_estimate=cost(10**10, near_list.size * 8),
        name="slots",
    )(near_list)


def near_kernel(slot_ref, own_ref, first_ref, second_ref, p_ref, o_ref, table, rhs):
    leaves = own_ref.shape[0] // LEAF
    width = own_ref.shape[1]
    for n, ref in enumerate((own_ref, first_ref, second_ref)):
        table[pl.ds(n * leaves, leaves)] = ref[...].reshape(leaves, LEAF, width)
    for i in range(leaves):
        rows = slice(i * LEAF, (i + 1) * LEAF)
        for j in range(NEAR):
            rhs[i % 2, j * LEAF : (j + 1) * LEAF] = table[slot_ref[i, j]]
        data = rhs[i % 2]
        straight = dot(p_ref[0, rows], data)
        crossed = dot(p_ref[1, rows], data)
        o_ref[rows] = straight + turn_lanes(crossed)


def near(slots, own, first, second, blocks):
    count, width = own.shape
    leaves = count // LEAF
    return pl.pallas_call(
        near_kernel,
        out_shape=jax.ShapeDtypeStruct((count, width), jnp.float32),
        in_specs=[SMEM, VMEM, VMEM, VMEM, VMEM],
        out_specs=VMEM,
        scratch_shapes=[
            pltpu.VMEM((3 * leaves, LEAF, width), jnp.bfloat16),
            pltpu.VMEM((2, NEAR * LEAF, width), jnp.bfloat16),
        ],
        compiler_params=params(4),
        cost_estimate=cost(4 * width * blocks.shape[1] * blocks.shape[2], blocks.size * 2),
        name="near",
    )(slots, own, first, second, blocks)


def mid_kernel(hops, a_ref, c_ref, *refs):
    *outs, rhs = refs
    for r in range(a_ref.shape[0]):
        lanes = slice(r * RANK, (r + 1) * RANK)
        rhs[0, :, lanes] = a_ref[r]
        rhs[1, :, lanes] = turn_rows(a_ref[r])
    for k, o_ref in zip(hops, outs):
        at = lax.axis_index("col") ^ k
        rows = pl.ds(pl.multiple_of(at * RANK, RANK), RANK)
        total = lax.dot_general(c_ref[0, rows], rhs[0], NT, preferred_element_type=jnp.float32)
        total += lax.dot_general(c_ref[1, rows], rhs[1], NT, preferred_element_type=jnp.float32)
        o_ref[...] = total.astype(jnp.bfloat16)


def mid(hops, arrived, coupling):
    groups, width, _ = arrived.shape
    share = len(hops) * RANK * coupling.shape[2]
    return pl.pallas_call(
        functools.partial(mid_kernel, hops),
        out_shape=[jax.ShapeDtypeStruct((RANK, width), jnp.bfloat16)] * len(hops),
        in_specs=[VMEM, VMEM],
        out_specs=[VMEM] * len(hops),
        scratch_shapes=[pltpu.VMEM((2, width, groups * RANK), jnp.bfloat16)],
        compiler_params=params(4),
        cost_estimate=cost(4 * width * share, share * 4),
        name="mid",
    )(arrived, coupling)


def far_kernel(hops, *refs):
    landed, (u_ref, n_ref, o_ref, data) = refs[: len(hops)], refs[len(hops) :]
    me = lax.axis_index("col")
    for n, k in enumerate(hops):
        at = pl.ds(pl.multiple_of((n & ~1) * RANK + ((me ^ k) & 1) * RANK, RANK), RANK)
        value = landed[n][...]
        data[0, at] = value
        data[1, at] = turn_lanes(value.astype(jnp.float32)).astype(jnp.bfloat16)
    step = 2 * RANK
    for i in range(0, n_ref.shape[0], step):
        rows = slice(i, i + step)
        total = n_ref[rows]
        for n in range(0, len(hops), 2):
            lanes = pl.ds(pl.multiple_of(((me ^ hops[n]) & ~1) * RANK, 2 * RANK), 2 * RANK)
            at = slice(n * RANK, (n + 2) * RANK)
            total += dot(u_ref[0, rows, lanes], data[0, at]) + dot(u_ref[1, rows, lanes], data[1, at])
        o_ref[rows] = total.astype(o_ref.dtype)


def far(hops, landed, factors, near_field, kind):
    count, width = near_field.shape
    share = len(hops) * RANK * count
    return pl.pallas_call(
        functools.partial(far_kernel, hops),
        out_shape=jax.ShapeDtypeStruct((count, width), kind),
        in_specs=[VMEM] * (len(hops) + 2),
        out_specs=VMEM,
        scratch_shapes=[pltpu.VMEM((2, len(hops) * RANK, width), jnp.bfloat16)],
        compiler_params=params(4),
        cost_estimate=cost(4 * width * share, share * 4),
        name="far",
    )(*landed, factors, near_field)


def stages(excitation, near_list, near_blocks, col_factors, coupling, row_factors):
    row_count = lax.axis_size("row")
    col_count = lax.axis_size("col")
    total = row_count * col_count
    axes = ("row", "col")
    inner = [(i, i ^ 1) for i in range(total)]
    outer = [(i, ((i + 1) ^ 1) - 1) for i in range(1, total - 1)]
    second = lax.ppermute(excitation, axes, outer)
    first = lax.ppermute(excitation, axes, inner)
    compressed = project(excitation, col_factors)
    arrived = lax.all_to_all(compressed, "row", split_axis=0, concat_axis=0, tiled=True)
    slots = slots_of(near_list)
    early = list(range(2, col_count))
    late = [1, 0]
    sent = dict(zip(early, mid(early, arrived, coupling)))
    sent.update(zip(late, mid(late, arrived, coupling)))
    landed = {0: sent[0]}
    for k in reversed(range(1, col_count)):
        landed[k] = lax.ppermute(sent[k], "col", [(i, i ^ k) for i in range(col_count)])
    total = near(slots, excitation, first, second, near_blocks)
    total = far([0, 1], [landed[0], landed[1]], row_factors, total, jnp.float32)
    return far(early, [landed[k] for k in early], row_factors, total, jnp.bfloat16)


def solution(mesh):
    return jax.shard_map(
        stages,
        mesh=mesh,
        in_specs=(
            P(("row", "col"), None),
            P(("row", "col"), None),
            P(None, ("row", "col"), None),
            P(None, ("row", "col"), None),
            P(None, ("row", "col"), None),
            P(None, ("row", "col"), None),
        ),
        out_specs=P(("row", "col"), None),
        check_vma=False,
    )
```

time: 29.5 us -> 30.4 us (1.031)
  local copies, waits for them, and re-layouts: 4.76 us -> 0.03 us
  Pallas kernels: 5.65 us -> 7.8 us
  starting transfers between devices: 10.9 us -> 12.8 us
  waiting for transfers between devices: 7.77 us -> 9.44 us
    unnamed x14 -> x10, local copies, waits for them, and re-layouts: 4.75 us -> 0.03 us
    all_to_all x1, starting transfers between devices: 7.54 us -> 9.64 us  [stages(): lax.all_to_all(compressed, 'row', split_axis=0, concat_axis=0, tiled=True)]
    pallas_call x1, Pallas kernels: 1.5 us -> 3.55 us  [project(): pl.pallas_call(project_kernel, out_shape=jax.ShapeDtypeStruct((groups, wi...]
    all_to_all x1, waiting for transfers between devices: 7.56 us -> 9.19 us  [stages(): lax.all_to_all(compressed, 'row', split_axis=0, concat_axis=0, tiled=True)]
    pallas_call x2 -> x5, Pallas kernels: 2.25 us -> 2.69 us  [the longest x2 1.74 us: far(): pl.pallas_call(functools.partial(far_kernel, hops), out_shape=jax.ShapeDt...]
    pallas_call x1, Pallas kernels: 1.91 us -> 1.55 us  [near(): pl.pallas_call(near_kernel, out_shape=jax.ShapeDtypeStruct((count, width)...]
  transfers between devices with their start and end apart: 6 -> 6, of which waited for: 2 -> 2; matrix products, arithmetic and copies ran while one was open for 0% -> 0% of each run, Pallas kernels for 9% -> 22%
where the time goes in v2:
time: 30.4 us; the launch traced here: 30.2 us
  starting transfers between devices  12.8 us (42%)
  waiting for transfers between devices  9.44 us (31%)
  Pallas kernels  7.8 us (26%)
    all_to_all x1, starting transfers between devices, stages(): lax.all_to_all(compressed, 'row', split_axis=0, concat_axis=0, tiled=True)  9.64 us
    all_to_all x1, waiting for transfers between devices, stages(): lax.all_to_all(compressed, 'row', split_axis=0, concat_axis=0, tiled=True)  9.19 us
    pallas_call x1, Pallas kernels, project(): pl.pallas_call(project_kernel, out_shape=jax.ShapeDtypeStruct((groups, wi...  3.55 us
    ppermute x3, starting transfers between devices, stages(): lax.ppermute(sent[k], 'col', [(i, i ^ k) for i in range(col_count)])  1.98 us
    pallas_call x2, Pallas kernels, far(): pl.pallas_call(functools.partial(far_kernel, hops), out_shape=jax.ShapeDt...  1.74 us
    pallas_call x1, Pallas kernels, near(): pl.pallas_call(near_kernel, out_shape=jax.ShapeDtypeStruct((count, width)...  1.55 us
    pallas_call x2, Pallas kernels, mid(): pl.pallas_call(functools.partial(mid_kernel, hops), out_shape=[jax.ShapeD...  0.94 us
    ppermute x1, starting transfers between devices, stages(): second = lax.ppermute(excitation, axes, outer)  0.67 us
  transfers between devices with their start and end apart: 6, of which 2 were waited for; matrix products, arithmetic and copies ran while one was open for 0% of the time, Pallas kernels for 22%

profile of v2, /device:TPU:0, one launch (start us, length us, event | category | flops | bytes accessed | tf_op | source)
XLA Modules:
  0.0 30.2 jit_solution(17246052202585839981)
XLA Ops:
  0.0 0.0 copy-start.4
  0.0 0.5 %collective-permute-start.3 = (bf16[1024,128]{1,0:T(8,128)(2,1)}, bf16[1024,128]{1,0:T(8,128)(2,1)S(1)}, u32[]{:S(2)}, u32[]{:S(2)}) collective-permute-start(bf16[1024,128]{1,0:T(8,128)(2,1)} %own_ref.1), channel_id=1, source_target_pairs={{0,1},{1,0},{2,3},{3,2},{4,5},{5,4},{6,7},{7,6},{8,9},{9,8},{10,11... | collective-permute-start | bytes 786440 | tf_op jit(solution)/shard_map/ppermute | solution.py:236
  0.5 0.7 %collective-permute-start.4 = (bf16[1024,128]{1,0:T(8,128)(2,1)}, bf16[1024,128]{1,0:T(8,128)(2,1)S(1)}, u32[]{:S(2)}, u32[]{:S(2)}) collective-permute-start(bf16[1024,128]{1,0:T(8,128)(2,1)} %own_ref.1), channel_id=1, source_target_pairs={{1,2},{2,1},{3,4},{4,3},{5,6},{6,5},{7,8},{8,7},{9,10},{10,9},{11,... | collective-permute-start | bytes 786440 | tf_op jit(solution)/shard_map/ppermute | solution.py:235
  1.2 3.6 %project.1 = bf16[8,128,128]{2,1,0:T(8,128)(2,1)} custom-call(bf16[1024,128]{1,0:T(8,128)(2,1)} %own_ref.1, bf16[2,1024,1024]{2,1,0:T(8,128)(2,1)} %v_hbm.1), custom_call_target="tpu_custom_call" | custom-call | flops 536870912 | bytes 4194304 | tf_op jit(solution)/shard_map/project/pallas_call | solution.py:89
  4.7 9.6 %all-to-all-start = ((bf16[8,128,128]{2,1,0:T(8,128)(2,1)}), bf16[8,128,128]{2,1,0:T(8,128)(2,1)S(1)}, u32[]{:S(2)}, u32[]{:S(2)}) async-start(bf16[8,128,128]{2,1,0:T(8,128)(2,1)} %project.1), calls=%async_computation | async-start | bytes 524288 | tf_op jit(solution)/shard_map/all_to_all | solution.py:238
  14.4 0.0 copy-done.4
  14.4 0.0 copy-start
  14.4 0.0 copy-start.3
  14.4 9.2 %all-to-all-done.a_ref = bf16[8,128,128]{2,1,0:T(8,128)(2,1)S(1)} async-done(((bf16[8,128,128]{2,1,0:T(8,128)(2,1)}), bf16[8,128,128]{2,1,0:T(8,128)(2,1)S(1)}, u32[]{:S(2)}, u32[]{:S(2)}) %all-to-all-start) | async-done | bytes 262176 | tf_op jit(solution)/shard_map/all_to_all | solution.py:238
  23.6 0.0 copy-done
  23.6 0.0 copy-start.2
  23.6 0.5 %mid.3 = (bf16[128,128]{1,0:T(8,128)(2,1)S(1)}, bf16[128,128]{1,0:T(8,128)(2,1)S(1)}) custom-call(bf16[8,128,128]{2,1,0:T(8,128)(2,1)S(1)} %all-to-all-done.a_ref, bf16[2,512,1024]{2,1,0:T(8,128)(2,1)S(1)} %copy-done), custom_call_target="tpu_custom_call" | custom-call | flops 134217728 | bytes 1048576 | tf_op jit(solution)/shard_map/mid/pallas_call | solution.py:182
  24.1 0.0 copy-start.1
  24.1 0.1 collective-permute-start.2
  24.2 0.5 %mid.2 = (bf16[128,128]{1,0:T(8,128)(2,1)S(1)}, bf16[128,128]{1,0:T(8,128)(2,1)S(1)}) custom-call(bf16[8,128,128]{2,1,0:T(8,128)(2,1)S(1)} %all-to-all-done.a_ref, bf16[2,512,1024]{2,1,0:T(8,128)(2,1)S(1)} %copy-done), custom_call_target="tpu_custom_call" | custom-call | flops 134217728 | bytes 1048576 | tf_op jit(solution)/shard_map/mid/pallas_call | solution.py:182
  24.7 0.6 %collective-permute-start = (bf16[128,128]{1,0:T(8,128)(2,1)S(1)}, bf16[128,128]{1,0:T(8,128)(2,1)S(1)}, u32[]{:S(2)}, u32[]{:S(2)}) collective-permute-start(bf16[128,128]{1,0:T(8,128)(2,1)S(1)} %get-tuple-element.9), channel_id=1, source_target_pairs={{0,2},{1,3},{2,0},{3,1},{4,6},{5,7},{6,4},{7,5},{8,10},{9,11},{10,... | collective-permute-start | bytes 98312 | tf_op jit(solution)/shard_map/ppermute | solution.py:246
  25.2 1.3 %collective-permute-start.1 = (bf16[128,128]{1,0:T(8,128)(2,1)S(1)}, bf16[128,128]{1,0:T(8,128)(2,1)S(1)}, u32[]{:S(2)}, u32[]{:S(2)}) collective-permute-start(bf16[128,128]{1,0:T(8,128)(2,1)S(1)} %get-tuple-element.10), channel_id=1, source_target_pairs={{0,3},{1,2},{2,1},{3,0},{4,7},{5,6},{6,5},{7,4},{8,11},{9,10},{10,... | collective-permute-start | bytes 98312 | tf_op jit(solution)/shard_map/ppermute | solution.py:246
  26.6 0.0 collective-permute-done.3.first_ref
  26.6 0.0 collective-permute-done.4.second_ref
  26.6 0.0 copy-done.3
  26.6 0.0 copy-done.2
  26.6 1.6 %near.1.refs_3_ = f32[1024,128]{1,0:T(8,128)S(1)} custom-call(s32[8,5]{1,0:T(8,128)S(1)} %slots.1.slot_ref, bf16[1024,128]{1,0:T(8,128)(2,1)S(1)} %copy-done.3, bf16[1024,128]{1,0:T(8,128)(2,1)S(1)} %collective-permute-done.3.first_ref, bf16[1024,128]{1,0:T(8,128)(2,1)S(1)} %collective-permute-done.4.second_ref, bf16[2,1024,640]{2,1,0:T(8,128)(2,1)S(1)} %copy-done.2), custom_call_target="tpu_custom_call" | custom-call | flops 335544320 | bytes 2621440 | tf_op jit(solution)/shard_map/near/pallas_call | solution.py:150
  28.2 0.0 collective-permute-done.2.refs_1_
  28.2 0.0 copy-done.1
  28.2 0.5 %far.2.refs_3_ = f32[1024,128]{1,0:T(8,128)S(1)} custom-call(bf16[128,128]{1,0:T(8,128)(2,1)S(1)} %get-tuple-element.11.refs_0_, bf16[128,128]{1,0:T(8,128)(2,1)S(1)} %collective-permute-done.2.refs_1_, bf16[2,1024,512]{2,1,0:T(8,128)(2,1)S(1)} %copy-done.1, f32[1024,128]{1,0:T(8,128)S(1)} %near.1.refs_3_), custom_call_target="tpu_custom_call" | custom-call | flops 134217728 | bytes 1048576 | tf_op jit(solution)/shard_map/far/pallas_call | solution.py:216
  28.7 0.2 collective-permute-done.refs_0_
  28.9 0.0 collective-permute-done.1.refs_1_
  28.9 1.2 %far.3 = bf16[1024,128]{1,0:T(8,128)(2,1)} custom-call(bf16[128,128]{1,0:T(8,128)(2,1)S(1)} %collective-permute-done.refs_0_, bf16[128,128]{1,0:T(8,128)(2,1)S(1)} %collective-permute-done.1.refs_1_, bf16[2,1024,512]{2,1,0:T(8,128)(2,1)S(1)} %copy-done.1, f32[1024,128]{1,0:T(8,128)S(1)} %far.2.refs_3_), custom_call_target="tpu_custom_call" | custom-call | flops 134217728 | bytes 1048576 | tf_op jit(solution)/shard_map/far/pallas_call | solution.py:216
  (1 shorter events, 0.0 us)
Async XLA Ops:
  0.0 14.4 %copy-start.4 = (s32[8,5]{1,0:T(8,128)S(1)}, s32[8,5]{1,0:T(8,128)}, u32[]{:S(2)}) copy-start(s32[8,5]{1,0:T(8,128)} %list_ref.1) | copy-start | bytes 484
  0.0 26.6 %collective-permute-start.3 = (bf16[1024,128]{1,0:T(8,128)(2,1)}, bf16[1024,128]{1,0:T(8,128)(2,1)S(1)}, u32[]{:S(2)}, u32[]{:S(2)}) collective-permute-start(bf16[1024,128]{1,0:T(8,128)(2,1)} %own_ref.1), channel_id=1, source_target_pairs={{0,1},{1,0},{2,3},{3,2},{4,5},{5,4},{6,7},{7,6},{8,9},{9,8},{10,11... | collective-permute-start | bytes 786440 | tf_op jit(solution)/shard_map/ppermute | solution.py:236
  0.5 26.1 %collective-permute-start.4 = (bf16[1024,128]{1,0:T(8,128)(2,1)}, bf16[1024,128]{1,0:T(8,128)(2,1)S(1)}, u32[]{:S(2)}, u32[]{:S(2)}) collective-permute-start(bf16[1024,128]{1,0:T(8,128)(2,1)} %own_ref.1), channel_id=1, source_target_pairs={{1,2},{2,1},{3,4},{4,3},{5,6},{6,5},{7,8},{8,7},{9,10},{10,9},{11,... | collective-permute-start | bytes 786440 | tf_op jit(solution)/shard_map/ppermute | solution.py:235
  4.7 18.9 %all-to-all-start = ((bf16[8,128,128]{2,1,0:T(8,128)(2,1)}), bf16[8,128,128]{2,1,0:T(8,128)(2,1)S(1)}, u32[]{:S(2)}, u32[]{:S(2)}) async-start(bf16[8,128,128]{2,1,0:T(8,128)(2,1)} %project.1), calls=%async_computation | async-start | bytes 524288 | tf_op jit(solution)/shard_map/all_to_all | solution.py:238
  14.4 9.2 %copy-start = (bf16[2,512,1024]{2,1,0:T(8,128)(2,1)S(1)}, bf16[2,512,1024]{2,1,0:T(8,128)(2,1)}, u32[]{:S(2)}) copy-start(bf16[2,512,1024]{2,1,0:T(8,128)(2,1)} %c_ref.3) | copy-start | bytes 6291460
  14.4 12.2 %copy-start.3 = (bf16[1024,128]{1,0:T(8,128)(2,1)S(1)}, bf16[1024,128]{1,0:T(8,128)(2,1)}, u32[]{:S(2)}) copy-start(bf16[1024,128]{1,0:T(8,128)(2,1)} %own_ref.1) | copy-start | bytes 786436
  23.6 3.0 %copy-start.2 = (bf16[2,1024,640]{2,1,0:T(8,128)(2,1)S(1)}, bf16[2,1024,640]{2,1,0:T(8,128)(2,1)}, u32[]{:S(2)}) copy-start(bf16[2,1024,640]{2,1,0:T(8,128)(2,1)} %p_ref.1) | copy-start | bytes 7864324
  24.1 4.1 %copy-start.1 = (bf16[2,1024,512]{2,1,0:T(8,128)(2,1)S(1)}, bf16[2,1024,512]{2,1,0:T(8,128)(2,1)}, u32[]{:S(2)}) copy-start(bf16[2,1024,512]{2,1,0:T(8,128)(2,1)} %refs_2_.3) | copy-start | bytes 6291460
  24.1 4.1 %collective-permute-start.2 = (bf16[128,128]{1,0:T(8,128)(2,1)S(1)}, bf16[128,128]{1,0:T(8,128)(2,1)S(1)}, u32[]{:S(2)}, u32[]{:S(2)}) collective-permute-start(bf16[128,128]{1,0:T(8,128)(2,1)S(1)} %get-tuple-element.12), channel_id=1, source_target_pairs={{0,1},{1,0},{2,3},{3,2},{4,5},{5,4},{6,7},{7,6},{8,9},{9,8},{10,11... | collective-permute-start | bytes 98312 | tf_op jit(solution)/shard_map/ppermute | solution.py:246
  24.7 4.3 %collective-permute-start = (bf16[128,128]{1,0:T(8,128)(2,1)S(1)}, bf16[128,128]{1,0:T(8,128)(2,1)S(1)}, u32[]{:S(2)}, u32[]{:S(2)}) collective-permute-start(bf16[128,128]{1,0:T(8,128)(2,1)S(1)} %get-tuple-element.9), channel_id=1, source_target_pairs={{0,2},{1,3},{2,0},{3,1},{4,6},{5,7},{6,4},{7,5},{8,10},{9,11},{10,... | collective-permute-start | bytes 98312 | tf_op jit(solution)/shard_map/ppermute | solution.py:246
  25.2 3.7 %collective-permute-start.1 = (bf16[128,128]{1,0:T(8,128)(2,1)S(1)}, bf16[128,128]{1,0:T(8,128)(2,1)S(1)}, u32[]{:S(2)}, u32[]{:S(2)}) collective-permute-start(bf16[128,128]{1,0:T(8,128)(2,1)S(1)} %get-tuple-element.10), channel_id=1, source_target_pairs={{0,3},{1,2},{2,1},{3,0},{4,7},{5,6},{6,5},{7,4},{8,11},{9,10},{10,... | collective-permute-start | bytes 98312 | tf_op jit(solution)/shard_map/ppermute | solution.py:246

commit v3 on v2

--- a/solution.py
+++ b/solution.py
@@ -18,7 +18,7 @@
 
 
 def params(mib):
-    return pltpu.CompilerParams(vmem_limit_bytes=mib * MIB)
+    return pltpu.CompilerParams(vmem_limit_bytes=int(mib * MIB))
 
 
 def cost(flops, moved):
@@ -41,7 +41,8 @@
     return jnp.where(lane < half, -rolled, rolled)
 
 
-def project_kernel(x_hbm, v_hbm, o_hbm, x_ref, v_ref, lhs, part, o_ref, x_sem, v_sem, o_sem):
+def project_kernel(x_hbm, v_hbm, own_ref, cross_ref, x_ref, v_ref, lhs, part, x_sem, v_sem):
+    row = lax.axis_index("row")
     half = x_ref.shape[0] // 2
     wide = 2 * RANK
     pieces = v_ref.shape[2] // wide
@@ -49,10 +50,6 @@
     def fetch(k, p):
         rows = pl.ds(k * half, half)
         return pltpu.make_async_copy(v_hbm.at[p, rows], v_ref.at[p, rows], v_sem.at[k, p])
-
-    def leave(n):
-        rows = pl.ds(n * 2, 2)
-        return pltpu.make_async_copy(o_ref.at[rows], o_hbm.at[rows], o_sem.at[n])
 
     def product(k, n):
         rows = slice(k * half, (k + 1) * half)
@@ -75,12 +72,11 @@
     for p in range(2):
         fetch(1, p).wait()
     for n in range(pieces):
-        total = part[n] + product(1, n)
-        for s in range(2):
-            o_ref[n * 2 + s] = total[:, s * RANK : (s + 1) * RANK].astype(jnp.bfloat16)
-        leave(n).start()
-    for n in range(pieces):
-        leave(n).wait()
+        total = (part[n] + product(1, n)).astype(jnp.bfloat16)
+        first, second = total[:, :RANK], total[:, RANK:]
+        at = n ^ (row // 2)
+        own_ref[at] = jnp.where(row % 2 == 0, first, second)
+        cross_ref[at] = jnp.where(row % 2 == 0, second, first)
 
 
 def project(x, v):
@@ -88,20 +84,18 @@
     count, width = x.shape
     return pl.pallas_call(
         project_kernel,
-        out_shape=jax.ShapeDtypeStruct((groups, width, RANK), jnp.bfloat16),
+        out_shape=[jax.ShapeDtypeStruct((groups // 2, width, RANK), jnp.bfloat16)] * 2,
         in_specs=[HBM, HBM],
-        out_specs=HBM,
+        out_specs=[VMEM, VMEM],
         scratch_shapes=[
             pltpu.VMEM(x.shape, x.dtype),
             pltpu.VMEM(v.shape, v.dtype),
             pltpu.VMEM((2, width, count), v.dtype),
             pltpu.VMEM((groups // 2, width, 2 * RANK), jnp.float32),
-            pltpu.VMEM((groups, width, RANK), v.dtype),
             pltpu.SemaphoreType.DMA(()),
             pltpu.SemaphoreType.DMA((2, 2)),
-            pltpu.SemaphoreType.DMA((groups // 2,)),
         ],
-        compiler_params=params(60),
+        compiler_params=params(53.6),
         cost_estimate=cost(4 * width * v.shape[1] * v.shape[2], v.size * 2),
         name="project",
     )(x, v)
@@ -129,11 +123,22 @@
     )(near_list)
 
 
-def near_kernel(slot_ref, own_ref, first_ref, second_ref, p_ref, o_ref, table, rhs):
+def near_kernel(slot_ref, own_ref, first_ref, second_ref, third_ref, p_ref, o_ref, table, rhs):
     leaves = own_ref.shape[0] // LEAF
     width = own_ref.shape[1]
-    for n, ref in enumerate((own_ref, first_ref, second_ref)):
+    for n, ref in enumerate((own_ref, first_ref)):
         table[pl.ds(n * leaves, leaves)] = ref[...].reshape(leaves, LEAF, width)
+    col = lax.axis_index("col")
+    edge = (col == 0) | (col == lax.axis_size("col") - 1)
+
+    @pl.when(edge)
+    def _():
+        table[pl.ds(2 * leaves, leaves)] = third_ref[...].reshape(leaves, LEAF, width)
+
+    @pl.when(jnp.logical_not(edge))
+    def _():
+        table[pl.ds(2 * leaves, leaves)] = second_ref[...].reshape(leaves, LEAF, width)
+
     for i in range(leaves):
         rows = slice(i * LEAF, (i + 1) * LEAF)
         for j in range(NEAR):
@@ -144,13 +149,13 @@
         o_ref[rows] = straight + turn_lanes(crossed)
 
 
-def near(slots, own, first, second, blocks):
+def near(slots, own, first, second, third, blocks):
     count, width = own.shape
     leaves = count // LEAF
     return pl.pallas_call(
         near_kernel,
         out_shape=jax.ShapeDtypeStruct((count, width), jnp.float32),
-        in_specs=[SMEM, VMEM, VMEM, VMEM, VMEM],
+        in_specs=[SMEM] + [VMEM] * 5,
         out_specs=VMEM,
         scratch_shapes=[
             pltpu.VMEM((3 * leaves, LEAF, width), jnp.bfloat16),
@@ -159,15 +164,40 @@
         compiler_params=params(4),
         cost_estimate=cost(4 * width * blocks.shape[1] * blocks.shape[2], blocks.size * 2),
         name="near",
-    )(slots, own, first, second, blocks)
-
-
-def mid_kernel(hops, a_ref, c_ref, *refs):
-    *outs, rhs = refs
-    for r in range(a_ref.shape[0]):
-        lanes = slice(r * RANK, (r + 1) * RANK)
-        rhs[0, :, lanes] = a_ref[r]
-        rhs[1, :, lanes] = turn_rows(a_ref[r])
+    )(slots, own, first, second, third, blocks)
+
+
+def pack_kernel(own_ref, got_ref, *outs):
+    for k, o_ref in enumerate(outs):
+        o_ref[0] = own_ref[k + 1]
+        o_ref[1] = got_ref[k + 1]
+
+
+def pack(own, got):
+    count = own.shape[0] - 1
+    return pl.pallas_call(
+        pack_kernel,
+        out_shape=[jax.ShapeDtypeStruct((2, *own.shape[1:]), own.dtype)] * count,
+        in_specs=[VMEM, VMEM],
+        out_specs=[VMEM] * count,
+        compiler_params=params(1),
+        cost_estimate=cost(0, own.size * 8),
+        name="pack",
+    )(own, got)
+
+
+def mid_kernel(hops, own_ref, got_ref, *refs):
+    half = own_ref.shape[0]
+    arrived, c_ref, outs, rhs = refs[: half - 1], refs[half - 1], refs[half:-1], refs[-1]
+    row = lax.axis_index("row")
+    for k in range(2 * half):
+        at = pl.ds(pl.multiple_of((row ^ k) * RANK, RANK), RANK)
+        if k < 2:
+            value = (own_ref, got_ref)[k][0]
+        else:
+            value = arrived[k // 2 - 1][k % 2]
+        rhs[0, :, at] = value
+        rhs[1, :, at] = turn_rows(value)
     for k, o_ref in zip(hops, outs):
         at = lax.axis_index("col") ^ k
         rows = pl.ds(pl.multiple_of(at * RANK, RANK), RANK)
@@ -176,19 +206,19 @@
         o_ref[...] = total.astype(jnp.bfloat16)
 
 
-def mid(hops, arrived, coupling):
-    groups, width, _ = arrived.shape
+def mid(hops, own, got, arrived, coupling):
+    half, width, _ = own.shape
     share = len(hops) * RANK * coupling.shape[2]
     return pl.pallas_call(
         functools.partial(mid_kernel, hops),
         out_shape=[jax.ShapeDtypeStruct((RANK, width), jnp.bfloat16)] * len(hops),
-        in_specs=[VMEM, VMEM],
+        in_specs=[VMEM] * (half + 2),
         out_specs=[VMEM] * len(hops),
-        scratch_shapes=[pltpu.VMEM((2, width, groups * RANK), jnp.bfloat16)],
+        scratch_shapes=[pltpu.VMEM((2, width, 2 * half * RANK), jnp.bfloat16)],
         compiler_params=params(4),
         cost_estimate=cost(4 * width * share, share * 4),
         name="mid",
-    )(arrived, coupling)
+    )(own, got, *arrived, coupling)
 
 
 def far_kernel(hops, *refs):
@@ -231,20 +261,28 @@
     total = row_count * col_count
     axes = ("row", "col")
     inner = [(i, i ^ 1) for i in range(total)]
-    outer = [(i, ((i + 1) ^ 1) - 1) for i in range(1, total - 1)]
+    outer, edge = [], []
+    for i in range(1, total - 1):
+        j = ((i + 1) ^ 1) - 1
+        (outer if i // col_count == j // col_count else edge).append((i, j))
+    third = lax.ppermute(excitation, axes, edge)
     second = lax.ppermute(excitation, axes, outer)
     first = lax.ppermute(excitation, axes, inner)
-    compressed = project(excitation, col_factors)
-    arrived = lax.all_to_all(compressed, "row", split_axis=0, concat_axis=0, tiled=True)
+    own, cross = project(excitation, col_factors)
+    got = lax.ppermute(cross, "row", [(i, i ^ 1) for i in range(row_count)])
+    sent = pack(own, got)
+    arrived = []
+    for k in range(1, row_count // 2):
+        arrived.append(lax.ppermute(sent[k - 1], "row", [(i, i ^ (2 * k)) for i in range(row_count)]))
     slots = slots_of(near_list)
     early = list(range(2, col_count))
     late = [1, 0]
-    sent = dict(zip(early, mid(early, arrived, coupling)))
-    sent.update(zip(late, mid(late, arrived, coupling)))
+    sent = dict(zip(early, mid(early, own, got, arrived, coupling)))
+    sent.update(zip(late, mid(late, own, got, arrived, coupling)))
     landed = {0: sent[0]}
     for k in reversed(range(1, col_count)):
         landed[k] = lax.ppermute(sent[k], "col", [(i, i ^ k) for i in range(col_count)])
-    total = near(slots, excitation, first, second, near_blocks)
+    total = near(slots, excitation, first, second, third, near_blocks)
     total = far([0, 1], [landed[0], landed[1]], row_factors, total, jnp.float32)
     return far(early, [landed[k] for k in early], row_factors, total, jnp.bfloat16)
 

time: 30.4 us -> 34.4 us (1.13)
  starting transfers between devices: 12.8 us -> 17.2 us
    ppermute x0 -> x5, starting transfers between devices: none -> 11.6 us  [the longest x3 7.95 us: stages(): lax.ppermute(sent[k - 1], 'row', [(i, i ^ 2 * k) for i in range(row_count)])]
    all_to_all x1 -> x0, starting transfers between devices: 9.64 us -> none  [stages(): lax.all_to_all(compressed, 'row', split_axis=0, concat_axis=0, tiled=True)]
    ppermute x0 -> x5, waiting for transfers between devices: none -> 9.23 us  [the longest x3 5.73 us: stages(): lax.ppermute(sent[k - 1], 'row', [(i, i ^ 2 * k) for i in range(row_count)])]
    all_to_all x1 -> x0, waiting for transfers between devices: 9.19 us -> none  [stages(): lax.all_to_all(compressed, 'row', split_axis=0, concat_axis=0, tiled=True)]
    ppermute x1, starting transfers between devices: 0.49 us -> 2.93 us  [stages(): first = lax.ppermute(excitation, axes, inner)]
    pallas_call x1 -> x2, Pallas kernels: 3.55 us -> 3.05 us  [the longest x1 3.03 us: project(): pl.pallas_call(project_kernel, out_shape=[jax.ShapeDtypeStruct((groups //...]
  transfers between devices with their start and end apart: 6 -> 10, of which waited for: 2 -> 4; matrix products, arithmetic and copies ran while one was open for 0% -> 0% of each run, Pallas kernels for 22% -> 10%
where the time goes in v3:
time: 34.4 us; the launch traced here: 34.3 us
  starting transfers between devices  17.2 us (50%)
  waiting for transfers between devices  9.33 us (27%)
  Pallas kernels  7.58 us (22%)
    ppermute x3, starting transfers between devices, stages(): lax.ppermute(sent[k - 1], 'row', [(i, i ^ 2 * k) for i in range(row_count)])  7.95 us
    ppermute x3, waiting for transfers between devices, stages(): lax.ppermute(sent[k - 1], 'row', [(i, i ^ 2 * k) for i in range(row_count)])  5.73 us
    ppermute x1, waiting for transfers between devices, stages(): got = lax.ppermute(cross, 'row', [(i, i ^ 1) for i in range(row_count)])  3.5 us
    pallas_call x1, Pallas kernels, project(): pl.pallas_call(project_kernel, out_shape=[jax.ShapeDtypeStruct((groups //...  3.03 us
    ppermute x1, starting transfers between devices, stages(): got = lax.ppermute(cross, 'row', [(i, i ^ 1) for i in range(row_count)])  3.03 us
    ppermute x1, starting transfers between devices, stages(): first = lax.ppermute(excitation, axes, inner)  2.93 us
    ppermute x3, starting transfers between devices, stages(): lax.ppermute(sent[k], 'col', [(i, i ^ k) for i in range(col_count)])  1.97 us
    pallas_call x2, Pallas kernels, far(): pl.pallas_call(functools.partial(far_kernel, hops), out_shape=jax.ShapeDt...  1.75 us
  transfers between devices with their start and end apart: 10, of which 4 were waited for; matrix products, arithmetic and copies ran while one was open for 0% of the time, Pallas kernels for 10%

profile of v3, /device:TPU:0, one launch (start us, length us, event | category | flops | bytes accessed | tf_op | source)
XLA Modules:
  0.0 34.3 jit_solution(12857874116313265955)
XLA Ops:
  0.0 3.0 %project.1 = (bf16[4,128,128]{2,1,0:T(8,128)(2,1)S(1)}, bf16[4,128,128]{2,1,0:T(8,128)(2,1)S(1)}) custom-call(bf16[1024,128]{1,0:T(8,128)(2,1)} %own_ref.1, bf16[2,1024,1024]{2,1,0:T(8,128)(2,1)} %v_hbm.1), custom_call_target="tpu_custom_call" | custom-call | flops 536870912 | bytes 4194304 | tf_op jit(solution)/shard_map/project/pallas_call | solution.py:85
  3.0 3.0 %collective-permute-start = (bf16[4,128,128]{2,1,0:T(8,128)(2,1)S(1)}, bf16[4,128,128]{2,1,0:T(8,128)(2,1)S(1)}, u32[]{:S(2)}, u32[]{:S(2)}) collective-permute-start(bf16[4,128,128]{2,1,0:T(8,128)(2,1)S(1)} %get-tuple-element.15), channel_id=1, source_target_pairs={{0,4},{4,0},{8,12},{12,8},{16,20},{20,16},{24,28},{28,24},{1,5},{5... | collective-permute-start | bytes 393224 | tf_op jit(solution)/shard_map/ppermute | solution.py:272
  6.1 3.5 %collective-permute-done.got_ref = bf16[4,128,128]{2,1,0:T(8,128)(2,1)S(1)} collective-permute-done((bf16[4,128,128]{2,1,0:T(8,128)(2,1)S(1)}, bf16[4,128,128]{2,1,0:T(8,128)(2,1)S(1)}, u32[]{:S(2)}, u32[]{:S(2)}) %collective-permute-start) | collective-permute-done | bytes 131104 | tf_op jit(solution)/shard_map/ppermute | solution.py:272
  9.6 1.9 %collective-permute-start.1 = (bf16[2,128,128]{2,1,0:T(8,128)(2,1)S(1)}, bf16[2,128,128]{2,1,0:T(8,128)(2,1)S(1)}, u32[]{:S(2)}, u32[]{:S(2)}) collective-permute-start(bf16[2,128,128]{2,1,0:T(8,128)(2,1)S(1)} %get-tuple-element.16), channel_id=1, source_target_pairs={{0,8},{4,12},{8,0},{12,4},{16,24},{20,28},{24,16},{28,20},{1,9},{5... | collective-permute-start | bytes 196616 | tf_op jit(solution)/shard_map/ppermute | solution.py:276
  11.5 0.0 copy-done.3
  11.5 0.7 %collective-permute-start.8 = (bf16[1024,128]{1,0:T(8,128)(2,1)S(1)}, bf16[1024,128]{1,0:T(8,128)(2,1)S(1)}, u32[]{:S(2)}, u32[]{:S(2)}) collective-permute-start(bf16[1024,128]{1,0:T(8,128)(2,1)S(1)} %copy-done.3), channel_id=1, source_target_pairs={{1,2},{2,1},{5,6},{6,5},{9,10},{10,9},{13,14},{14,13},{17,18},{18,... | collective-permute-start | bytes 786440 | tf_op jit(solution)/shard_map/ppermute | solution.py:269
  12.2 2.9 %collective-permute-start.7 = (bf16[1024,128]{1,0:T(8,128)(2,1)S(1)}, bf16[1024,128]{1,0:T(8,128)(2,1)S(1)}, u32[]{:S(2)}, u32[]{:S(2)}) collective-permute-start(bf16[1024,128]{1,0:T(8,128)(2,1)S(1)} %copy-done.3), channel_id=1, source_target_pairs={{0,1},{1,0},{2,3},{3,2},{4,5},{5,4},{6,7},{7,6},{8,9},{9,8},{10,11... | collective-permute-start | bytes 786440 | tf_op jit(solution)/shard_map/ppermute | solution.py:270
  15.1 0.7 %collective-permute-start.9 = (bf16[1024,128]{1,0:T(8,128)(2,1)S(1)}, bf16[1024,128]{1,0:T(8,128)(2,1)S(1)}, u32[]{:S(2)}, u32[]{:S(2)}) collective-permute-start(bf16[1024,128]{1,0:T(8,128)(2,1)S(1)} %copy-done.3), channel_id=1, source_target_pairs={{3,4},{4,3},{7,8},{8,7},{11,12},{12,11},{15,16},{16,15},{19,20},{2... | collective-permute-start | bytes 786440 | tf_op jit(solution)/shard_map/ppermute | solution.py:268
  15.8 3.9 %collective-permute-start.2 = (bf16[2,128,128]{2,1,0:T(8,128)(2,1)S(1)}, bf16[2,128,128]{2,1,0:T(8,128)(2,1)S(1)}, u32[]{:S(2)}, u32[]{:S(2)}) collective-permute-start(bf16[2,128,128]{2,1,0:T(8,128)(2,1)S(1)} %get-tuple-element.17), channel_id=1, source_target_pairs={{0,16},{4,20},{8,24},{12,28},{16,0},{20,4},{24,8},{28,12},{1,17},{... | collective-permute-start | bytes 196616 | tf_op jit(solution)/shard_map/ppermute | solution.py:276
  19.7 0.0 collective-permute-done.1.refs_0_
  19.7 2.2 %collective-permute-start.3 = (bf16[2,128,128]{2,1,0:T(8,128)(2,1)S(1)}, bf16[2,128,128]{2,1,0:T(8,128)(2,1)S(1)}, u32[]{:S(2)}, u32[]{:S(2)}) collective-permute-start(bf16[2,128,128]{2,1,0:T(8,128)(2,1)S(1)} %get-tuple-element.18), channel_id=1, source_target_pairs={{0,24},{4,28},{8,16},{12,20},{16,8},{20,12},{24,0},{28,4},{1,25},{... | collective-permute-start | bytes 196616 | tf_op jit(solution)/shard_map/ppermute | solution.py:276
  21.8 0.0 copy-done.4
  21.8 0.0 copy-start.2
  21.9 3.7 %collective-permute-done.2.refs_1_ = bf16[2,128,128]{2,1,0:T(8,128)(2,1)S(1)} collective-permute-done((bf16[2,128,128]{2,1,0:T(8,128)(2,1)S(1)}, bf16[2,128,128]{2,1,0:T(8,128)(2,1)S(1)}, u32[]{:S(2)}, u32[]{:S(2)}) %collective-permute-start.2) | collective-permute-done | bytes 65568 | tf_op jit(solution)/shard_map/ppermute | solution.py:276
  25.6 2.0 %collective-permute-done.3.refs_2_ = bf16[2,128,128]{2,1,0:T(8,128)(2,1)S(1)} collective-permute-done((bf16[2,128,128]{2,1,0:T(8,128)(2,1)S(1)}, bf16[2,128,128]{2,1,0:T(8,128)(2,1)S(1)}, u32[]{:S(2)}, u32[]{:S(2)}) %collective-permute-start.3) | collective-permute-done | bytes 65568 | tf_op jit(solution)/shard_map/ppermute | solution.py:276
  27.6 0.0 copy-done
  27.6 0.6 %mid.3 = (bf16[128,128]{1,0:T(8,128)(2,1)S(1)}, bf16[128,128]{1,0:T(8,128)(2,1)S(1)}) custom-call(bf16[4,128,128]{2,1,0:T(8,128)(2,1)S(1)} %get-tuple-element.14.own_ref, bf16[4,128,128]{2,1,0:T(8,128)(2,1)S(1)} %collective-permute-done.got_ref, bf16[2,128,128]{2,1,0:T(8,128)(2,1)S(1)} %collective-permute-done.1.refs_0_, ...), custom_call_target="tpu_custom_call" | custom-call | flops 134217728 | bytes 1048576 | tf_op jit(solution)/shard_map/mid/pallas_call | solution.py:212
  28.2 0.1 collective-permute-start.6
  28.2 0.6 %mid.2 = (bf16[128,128]{1,0:T(8,128)(2,1)S(1)}, bf16[128,128]{1,0:T(8,128)(2,1)S(1)}) custom-call(bf16[4,128,128]{2,1,0:T(8,128)(2,1)S(1)} %get-tuple-element.14.own_ref, bf16[4,128,128]{2,1,0:T(8,128)(2,1)S(1)} %collective-permute-done.got_ref, bf16[2,128,128]{2,1,0:T(8,128)(2,1)S(1)} %collective-permute-done.1.refs_0_, ...), custom_call_target="tpu_custom_call" | custom-call | flops 134217728 | bytes 1048576 | tf_op jit(solution)/shard_map/mid/pallas_call | solution.py:212
  28.8 0.0 copy-start.1
  28.8 0.1 collective-permute-start.4
  28.9 0.0 collective-permute-done.8.second_ref
  28.9 1.8 %collective-permute-start.5 = (bf16[128,128]{1,0:T(8,128)(2,1)S(1)}, bf16[128,128]{1,0:T(8,128)(2,1)S(1)}, u32[]{:S(2)}, u32[]{:S(2)}) collective-permute-start(bf16[128,128]{1,0:T(8,128)(2,1)S(1)} %get-tuple-element.20), channel_id=1, source_target_pairs={{0,3},{1,2},{2,1},{3,0},{4,7},{5,6},{6,5},{7,4},{8,11},{9,10},{10,... | collective-permute-start | bytes 98312 | tf_op jit(solution)/shard_map/ppermute | solution.py:284
  30.7 0.0 collective-permute-done.7.first_ref
  30.8 0.0 collective-permute-done.9.third_ref
  30.8 0.0 copy-done.2
  30.8 1.6 %near.1.refs_3_ = f32[1024,128]{1,0:T(8,128)S(1)} custom-call(s32[8,5]{1,0:T(8,128)S(1)} %slots.1.slot_ref, bf16[1024,128]{1,0:T(8,128)(2,1)S(1)} %copy-done.3, bf16[1024,128]{1,0:T(8,128)(2,1)S(1)} %collective-permute-done.7.first_ref, bf16[1024,128]{1,0:T(8,128)(2,1)S(1)} %collective-permute-done.8.second_ref, ...), custom_call_target="tpu_custom_call" | custom-call | flops 335544320 | bytes 2621440 | tf_op jit(solution)/shard_map/near/pallas_call | solution.py:155
  32.4 0.0 collective-permute-done.6.refs_1_
  32.4 0.5 %far.2.refs_3_ = f32[1024,128]{1,0:T(8,128)S(1)} custom-call(bf16[128,128]{1,0:T(8,128)(2,1)S(1)} %get-tuple-element.21.refs_0_, bf16[128,128]{1,0:T(8,128)(2,1)S(1)} %collective-permute-done.6.refs_1_, bf16[2,1024,512]{2,1,0:T(8,128)(2,1)S(1)} %copy-done.1, f32[1024,128]{1,0:T(8,128)S(1)} %near.1.refs_3_), custom_call_target="tpu_custom_call" | custom-call | flops 134217728 | bytes 1048576 | tf_op jit(solution)/shard_map/far/pallas_call | solution.py:246
  32.9 0.1 collective-permute-done.4.refs_0_
  33.0 0.0 collective-permute-done.5.refs_1_
  33.0 1.2 %far.3 = bf16[1024,128]{1,0:T(8,128)(2,1)} custom-call(bf16[128,128]{1,0:T(8,128)(2,1)S(1)} %collective-permute-done.4.refs_0_, bf16[128,128]{1,0:T(8,128)(2,1)S(1)} %collective-permute-done.5.refs_1_, bf16[2,1024,512]{2,1,0:T(8,128)(2,1)S(1)} %copy-done.1, f32[1024,128]{1,0:T(8,128)S(1)} %far.2.refs_3_), custom_call_target="tpu_custom_call" | custom-call | flops 134217728 | bytes 1048576 | tf_op jit(solution)/shard_map/far/pallas_call | solution.py:246
  (6 shorter events, 0.0 us)
Async XLA Ops:
  0.0 11.5 %copy-start.3 = (bf16[1024,128]{1,0:T(8,128)(2,1)S(1)}, bf16[1024,128]{1,0:T(8,128)(2,1)}, u32[]{:S(2)}) copy-start(bf16[1024,128]{1,0:T(8,128)(2,1)} %own_ref.1) | copy-start | bytes 786436
  0.0 21.8 %copy-start.4 = (s32[8,5]{1,0:T(8,128)S(1)}, s32[8,5]{1,0:T(8,128)}, u32[]{:S(2)}) copy-start(s32[8,5]{1,0:T(8,128)} %list_ref.1) | copy-start | bytes 484
  3.0 6.5 %collective-permute-start = (bf16[4,128,128]{2,1,0:T(8,128)(2,1)S(1)}, bf16[4,128,128]{2,1,0:T(8,128)(2,1)S(1)}, u32[]{:S(2)}, u32[]{:S(2)}) collective-permute-start(bf16[4,128,128]{2,1,0:T(8,128)(2,1)S(1)} %get-tuple-element.15), channel_id=1, source_target_pairs={{0,4},{4,0},{8,12},{12,8},{16,20},{20,16},{24,28},{28,24},{1,5},{5... | collective-permute-start | bytes 393224 | tf_op jit(solution)/shard_map/ppermute | solution.py:272
  9.6 10.1 %collective-permute-start.1 = (bf16[2,128,128]{2,1,0:T(8,128)(2,1)S(1)}, bf16[2,128,128]{2,1,0:T(8,128)(2,1)S(1)}, u32[]{:S(2)}, u32[]{:S(2)}) collective-permute-start(bf16[2,128,128]{2,1,0:T(8,128)(2,1)S(1)} %get-tuple-element.16), channel_id=1, source_target_pairs={{0,8},{4,12},{8,0},{12,4},{16,24},{20,28},{24,16},{28,20},{1,9},{5... | collective-permute-start | bytes 196616 | tf_op jit(solution)/shard_map/ppermute | solution.py:276
  11.5 17.4 %collective-permute-start.8 = (bf16[1024,128]{1,0:T(8,128)(2,1)S(1)}, bf16[1024,128]{1,0:T(8,128)(2,1)S(1)}, u32[]{:S(2)}, u32[]{:S(2)}) collective-permute-start(bf16[1024,128]{1,0:T(8,128)(2,1)S(1)} %copy-done.3), channel_id=1, source_target_pairs={{1,2},{2,1},{5,6},{6,5},{9,10},{10,9},{13,14},{14,13},{17,18},{18,... | collective-permute-start | bytes 786440 | tf_op jit(solution)/shard_map/ppermute | solution.py:269
  12.2 18.6 %collective-permute-start.7 = (bf16[1024,128]{1,0:T(8,128)(2,1)S(1)}, bf16[1024,128]{1,0:T(8,128)(2,1)S(1)}, u32[]{:S(2)}, u32[]{:S(2)}) collective-permute-start(bf16[1024,128]{1,0:T(8,128)(2,1)S(1)} %copy-done.3), channel_id=1, source_target_pairs={{0,1},{1,0},{2,3},{3,2},{4,5},{5,4},{6,7},{7,6},{8,9},{9,8},{10,11... | collective-permute-start | bytes 786440 | tf_op jit(solution)/shard_map/ppermute | solution.py:270
  15.1 15.7 %collective-permute-start.9 = (bf16[1024,128]{1,0:T(8,128)(2,1)S(1)}, bf16[1024,128]{1,0:T(8,128)(2,1)S(1)}, u32[]{:S(2)}, u32[]{:S(2)}) collective-permute-start(bf16[1024,128]{1,0:T(8,128)(2,1)S(1)} %copy-done.3), channel_id=1, source_target_pairs={{3,4},{4,3},{7,8},{8,7},{11,12},{12,11},{15,16},{16,15},{19,20},{2... | collective-permute-start | bytes 786440 | tf_op jit(solution)/shard_map/ppermute | solution.py:268
  15.8 9.8 %collective-permute-start.2 = (bf16[2,128,128]{2,1,0:T(8,128)(2,1)S(1)}, bf16[2,128,128]{2,1,0:T(8,128)(2,1)S(1)}, u32[]{:S(2)}, u32[]{:S(2)}) collective-permute-start(bf16[2,128,128]{2,1,0:T(8,128)(2,1)S(1)} %get-tuple-element.17), channel_id=1, source_target_pairs={{0,16},{4,20},{8,24},{12,28},{16,0},{20,4},{24,8},{28,12},{1,17},{... | collective-permute-start | bytes 196616 | tf_op jit(solution)/shard_map/ppermute | solution.py:276
  19.7 7.9 %copy-start = (bf16[2,512,1024]{2,1,0:T(8,128)(2,1)S(1)}, bf16[2,512,1024]{2,1,0:T(8,128)(2,1)}, u32[]{:S(2)}) copy-start(bf16[2,512,1024]{2,1,0:T(8,128)(2,1)} %refs_3_.3) | copy-start | bytes 6291460
  19.7 7.9 %collective-permute-start.3 = (bf16[2,128,128]{2,1,0:T(8,128)(2,1)S(1)}, bf16[2,128,128]{2,1,0:T(8,128)(2,1)S(1)}, u32[]{:S(2)}, u32[]{:S(2)}) collective-permute-start(bf16[2,128,128]{2,1,0:T(8,128)(2,1)S(1)} %get-tuple-element.18), channel_id=1, source_target_pairs={{0,24},{4,28},{8,16},{12,20},{16,8},{20,12},{24,0},{28,4},{1,25},{... | collective-permute-start | bytes 196616 | tf_op jit(solution)/shard_map/ppermute | solution.py:276
  21.8 8.9 %copy-start.2 = (bf16[2,1024,640]{2,1,0:T(8,128)(2,1)S(1)}, bf16[2,1024,640]{2,1,0:T(8,128)(2,1)}, u32[]{:S(2)}) copy-start(bf16[2,1024,640]{2,1,0:T(8,128)(2,1)} %p_ref.1) | copy-start | bytes 7864324
  28.2 4.2 %collective-permute-start.6 = (bf16[128,128]{1,0:T(8,128)(2,1)S(1)}, bf16[128,128]{1,0:T(8,128)(2,1)S(1)}, u32[]{:S(2)}, u32[]{:S(2)}) collective-permute-start(bf16[128,128]{1,0:T(8,128)(2,1)S(1)} %get-tuple-element.22), channel_id=1, source_target_pairs={{0,1},{1,0},{2,3},{3,2},{4,5},{5,4},{6,7},{7,6},{8,9},{9,8},{10,11... | collective-permute-start | bytes 98312 | tf_op jit(solution)/shard_map/ppermute | solution.py:284
  28.8 3.6 %copy-start.1 = (bf16[2,1024,512]{2,1,0:T(8,128)(2,1)S(1)}, bf16[2,1024,512]{2,1,0:T(8,128)(2,1)}, u32[]{:S(2)}) copy-start(bf16[2,1024,512]{2,1,0:T(8,128)(2,1)} %refs_2_.3) | copy-start | bytes 6291460
  28.8 4.2 %collective-permute-start.4 = (bf16[128,128]{1,0:T(8,128)(2,1)S(1)}, bf16[128,128]{1,0:T(8,128)(2,1)S(1)}, u32[]{:S(2)}, u32[]{:S(2)}) collective-permute-start(bf16[128,128]{1,0:T(8,128)(2,1)S(1)} %get-tuple-element.19), channel_id=1, source_target_pairs={{0,2},{1,3},{2,0},{3,1},{4,6},{5,7},{6,4},{7,5},{8,10},{9,11},{10,... | collective-permute-start | bytes 98312 | tf_op jit(solution)/shard_map/ppermute | solution.py:284
  28.9 4.1 %collective-permute-start.5 = (bf16[128,128]{1,0:T(8,128)(2,1)S(1)}, bf16[128,128]{1,0:T(8,128)(2,1)S(1)}, u32[]{:S(2)}, u32[]{:S(2)}) collective-permute-start(bf16[128,128]{1,0:T(8,128)(2,1)S(1)} %get-tuple-element.20), channel_id=1, source_target_pairs={{0,3},{1,2},{2,1},{3,0},{4,7},{5,6},{6,5},{7,4},{8,11},{9,10},{10,... | collective-permute-start | bytes 98312 | tf_op jit(solution)/shard_map/ppermute | solution.py:284

commit v4 on v3

--- a/solution.py
+++ b/solution.py
@@ -123,70 +123,97 @@
     )(near_list)
 
 
-def near_kernel(slot_ref, own_ref, first_ref, second_ref, third_ref, p_ref, o_ref, table, rhs):
-    leaves = own_ref.shape[0] // LEAF
-    width = own_ref.shape[1]
-    for n, ref in enumerate((own_ref, first_ref)):
-        table[pl.ds(n * leaves, leaves)] = ref[...].reshape(leaves, LEAF, width)
+def table_kernel(own_ref, first_ref, o_ref):
+    count = own_ref.shape[0]
+    o_ref[:count] = own_ref[...]
+    o_ref[count : 2 * count] = first_ref[...]
+
+
+def table_of(own, first):
+    count, width = own.shape
+    return pl.pallas_call(
+        table_kernel,
+        out_shape=jax.ShapeDtypeStruct((3 * count, width), own.dtype),
+        in_specs=[VMEM, VMEM],
+        out_specs=VMEM,
+        compiler_params=params(1),
+        cost_estimate=cost(0, own.size * 8),
+        name="table",
+    )(own, first)
+
+
+def near_kernel(slot_ref, table_in, second_ref, third_ref, p_ref, o_ref, table, rhs):
+    count = second_ref.shape[0]
     col = lax.axis_index("col")
     edge = (col == 0) | (col == lax.axis_size("col") - 1)
 
     @pl.when(edge)
     def _():
-        table[pl.ds(2 * leaves, leaves)] = third_ref[...].reshape(leaves, LEAF, width)
+        table[2 * count :] = third_ref[...]
 
     @pl.when(jnp.logical_not(edge))
     def _():
-        table[pl.ds(2 * leaves, leaves)] = second_ref[...].reshape(leaves, LEAF, width)
-
-    for i in range(leaves):
+        table[2 * count :] = second_ref[...]
+
+    slots = slot_ref[...] * LEAF
+    for i in range(count // LEAF):
         rows = slice(i * LEAF, (i + 1) * LEAF)
         for j in range(NEAR):
-            rhs[i % 2, j * LEAF : (j + 1) * LEAF] = table[slot_ref[i, j]]
+            at = pl.ds(pl.multiple_of(slots[i, j], LEAF), LEAF)
+            rhs[i % 2, j * LEAF : (j + 1) * LEAF] = table[at]
         data = rhs[i % 2]
         straight = dot(p_ref[0, rows], data)
         crossed = dot(p_ref[1, rows], data)
         o_ref[rows] = straight + turn_lanes(crossed)
 
 
-def near(slots, own, first, second, third, blocks):
-    count, width = own.shape
-    leaves = count // LEAF
+def near(slots, table, second, third, blocks):
+    count, width = second.shape
     return pl.pallas_call(
         near_kernel,
-        out_shape=jax.ShapeDtypeStruct((count, width), jnp.float32),
-        in_specs=[SMEM] + [VMEM] * 5,
-        out_specs=VMEM,
-        scratch_shapes=[
-            pltpu.VMEM((3 * leaves, LEAF, width), jnp.bfloat16),
-            pltpu.VMEM((2, NEAR * LEAF, width), jnp.bfloat16),
+        out_shape=[
+            jax.ShapeDtypeStruct((count, width), jnp.float32),
+            jax.ShapeDtypeStruct(table.shape, table.dtype),
         ],
+        in_specs=[VMEM] * 5,
+        out_specs=[VMEM, VMEM],
+        input_output_aliases={1: 1},
+        scratch_shapes=[pltpu.VMEM((2, NEAR * LEAF, width), jnp.bfloat16)],
         compiler_params=params(4),
         cost_estimate=cost(4 * width * blocks.shape[1] * blocks.shape[2], blocks.size * 2),
         name="near",
-    )(slots, own, first, second, third, blocks)
-
-
-def pack_kernel(own_ref, got_ref, *outs):
-    for k, o_ref in enumerate(outs):
-        o_ref[0] = own_ref[k + 1]
-        o_ref[1] = got_ref[k + 1]
-
-
-def pack(own, got):
-    count = own.shape[0] - 1
-    return pl.pallas_call(
-        pack_kernel,
-        out_shape=[jax.ShapeDtypeStruct((2, *own.shape[1:]), own.dtype)] * count,
+    )(slots, table, second, third, blocks)[0]
+
+
+def pack_kernel(hops, own_ref, got_ref, *outs):
+    base = hops[-1] + 1 - got_ref.shape[0]
+    for k, o_ref in zip(hops, outs):
+        o_ref[0] = own_ref[k]
+        o_ref[1] = got_ref[k - base]
+
+
+def pack(hops, own, got):
+    return pl.pallas_call(
+        functools.partial(pack_kernel, hops),
+        out_shape=[jax.ShapeDtypeStruct((2, *own.shape[1:]), own.dtype)] * len(hops),
         in_specs=[VMEM, VMEM],
-        out_specs=[VMEM] * count,
+        out_specs=[VMEM] * len(hops),
         compiler_params=params(1),
-        cost_estimate=cost(0, own.size * 8),
-        name="pack",
+        cost_estimate=cost(0, len(hops) * own.size * 2),
+        name="pairs",
     )(own, got)
 
 
-def mid_kernel(hops, own_ref, got_ref, *refs):
+def couple(hops, c_ref, rhs, outs):
+    for k, o_ref in zip(hops, outs):
+        at = lax.axis_index("col") ^ k
+        rows = pl.ds(pl.multiple_of(at * RANK, RANK), RANK)
+        total = lax.dot_general(c_ref[0, rows], rhs[0], NT, preferred_element_type=jnp.float32)
+        total += lax.dot_general(c_ref[1, rows], rhs[1], NT, preferred_element_type=jnp.float32)
+        o_ref[...] = total.astype(jnp.bfloat16)
+
+
+def early_kernel(hops, own_ref, got_ref, *refs):
     half = own_ref.shape[0]
     arrived, c_ref, outs, rhs = refs[: half - 1], refs[half - 1], refs[half:-1], refs[-1]
     row = lax.axis_index("row")
@@ -198,27 +225,25 @@
             value = arrived[k // 2 - 1][k % 2]
         rhs[0, :, at] = value
         rhs[1, :, at] = turn_rows(value)
-    for k, o_ref in zip(hops, outs):
-        at = lax.axis_index("col") ^ k
-        rows = pl.ds(pl.multiple_of(at * RANK, RANK), RANK)
-        total = lax.dot_general(c_ref[0, rows], rhs[0], NT, preferred_element_type=jnp.float32)
-        total += lax.dot_general(c_ref[1, rows], rhs[1], NT, preferred_element_type=jnp.float32)
-        o_ref[...] = total.astype(jnp.bfloat16)
-
-
-def mid(hops, own, got, arrived, coupling):
-    half, width, _ = own.shape
+    couple(hops, c_ref, rhs, outs)
+
+
+def late_kernel(hops, rhs, c_ref, *outs):
+    couple(hops, c_ref, rhs, outs)
+
+
+def mid(kernel, hops, operands, coupling, extra):
+    width = operands[0].shape[1]
     share = len(hops) * RANK * coupling.shape[2]
     return pl.pallas_call(
-        functools.partial(mid_kernel, hops),
-        out_shape=[jax.ShapeDtypeStruct((RANK, width), jnp.bfloat16)] * len(hops),
-        in_specs=[VMEM] * (half + 2),
-        out_specs=[VMEM] * len(hops),
-        scratch_shapes=[pltpu.VMEM((2, width, 2 * half * RANK), jnp.bfloat16)],
+        functools.partial(kernel, hops),
+        out_shape=[jax.ShapeDtypeStruct((RANK, width), jnp.bfloat16)] * len(hops) + extra,
+        in_specs=[VMEM] * (len(operands) + 1),
+        out_specs=[VMEM] * (len(hops) + len(extra)),
         compiler_params=params(4),
         cost_estimate=cost(4 * width * share, share * 4),
         name="mid",
-    )(own, got, *arrived, coupling)
+    )(*operands, coupling)
 
 
 def far_kernel(hops, *refs):
@@ -269,20 +294,28 @@
     second = lax.ppermute(excitation, axes, outer)
     first = lax.ppermute(excitation, axes, inner)
     own, cross = project(excitation, col_factors)
-    got = lax.ppermute(cross, "row", [(i, i ^ 1) for i in range(row_count)])
-    sent = pack(own, got)
+    steps = row_count // 2
+    beyond, close = list(range(steps // 2, steps)), list(range(1, steps // 2))
+    aside = [(i, i ^ 1) for i in range(row_count)]
+    got_beyond = lax.ppermute(cross[steps // 2 :], "row", aside)
+    got = lax.ppermute(cross[: steps // 2], "row", aside)
+    sent = dict(zip(beyond, pack(beyond, own, got_beyond)))
+    sent.update(zip(close, pack(close, own, got)))
     arrived = []
-    for k in range(1, row_count // 2):
-        arrived.append(lax.ppermute(sent[k - 1], "row", [(i, i ^ (2 * k)) for i in range(row_count)]))
+    for k in range(1, steps):
+        arrived.append(lax.ppermute(sent[k], "row", [(i, i ^ (2 * k)) for i in range(row_count)]))
     slots = slots_of(near_list)
+    table = table_of(excitation, first)
     early = list(range(2, col_count))
     late = [1, 0]
-    sent = dict(zip(early, mid(early, own, got, arrived, coupling)))
-    sent.update(zip(late, mid(late, own, got, arrived, coupling)))
+    turned = jax.ShapeDtypeStruct((2, own.shape[1], coupling.shape[2]), own.dtype)
+    *blocks, rhs = mid(early_kernel, early, [own, got, *arrived], coupling, [turned])
+    sent = dict(zip(early, blocks))
+    sent.update(zip(late, mid(late_kernel, late, [rhs], coupling, [])))
     landed = {0: sent[0]}
     for k in reversed(range(1, col_count)):
         landed[k] = lax.ppermute(sent[k], "col", [(i, i ^ k) for i in range(col_count)])
-    total = near(slots, excitation, first, second, third, near_blocks)
+    total = near(slots, table, second, third, near_blocks)
     total = far([0, 1], [landed[0], landed[1]], row_factors, total, jnp.float32)
     return far(early, [landed[k] for k in early], row_factors, total, jnp.bfloat16)
 

time: 34.4 us -> 28.7 us (0.83)
  the two profiles are of different devices: /device:TPU:0 before, /device:TPU:6 now
where the time goes in v4:
time: 28.7 us; the launch traced here: 28.5 us
  starting transfers between devices  11.2 us (39%)
  waiting for transfers between devices  10.2 us (36%)
  Pallas kernels  6.93 us (24%)
    ppermute x1, waiting for transfers between devices, stages(): second = lax.ppermute(excitation, axes, outer)  5.47 us
    ppermute x3, starting transfers between devices, stages(): lax.ppermute(sent[k], 'row', [(i, i ^ 2 * k) for i in range(row_count)])  4.3 us
    pallas_call x1, Pallas kernels, project(): pl.pallas_call(project_kernel, out_shape=[jax.ShapeDtypeStruct((groups //...  3.03 us
    ppermute x1, waiting for transfers between devices, stages(): got_beyond = lax.ppermute(cross[steps // 2:], 'row', aside)  2.51 us
    ppermute x3, starting transfers between devices, stages(): lax.ppermute(sent[k], 'col', [(i, i ^ k) for i in range(col_count)])  2.22 us
    ppermute x3, waiting for transfers between devices, stages(): lax.ppermute(sent[k], 'row', [(i, i ^ 2 * k) for i in range(row_count)])  2.21 us
    ppermute x1, starting transfers between devices, stages(): second = lax.ppermute(excitation, axes, outer)  1.91 us
    pallas_call x2, Pallas kernels, far(): pl.pallas_call(functools.partial(far_kernel, hops), out_shape=jax.ShapeDt...  1.75 us
  transfers between devices with their start and end apart: 11, of which 3 were waited for; matrix products, arithmetic and copies ran while one was open for 0% of the time, Pallas kernels for 9%

profile of v4, /device:TPU:6, one launch (start us, length us, event | category | flops | bytes accessed | tf_op | source)
XLA Modules:
  0.0 28.5 jit_solution(4880364518066331079)
XLA Ops:
  0.0 3.0 %project.1 = (bf16[4,128,128]{2,1,0:T(8,128)(2,1)S(1)}, bf16[4,128,128]{2,1,0:T(8,128)(2,1)S(1)}) custom-call(bf16[1024,128]{1,0:T(8,128)(2,1)} %own_ref.1, bf16[2,1024,1024]{2,1,0:T(8,128)(2,1)} %v_hbm.1), custom_call_target="tpu_custom_call" | custom-call | flops 536870912 | bytes 4194304 | tf_op jit(solution)/shard_map/project/pallas_call | solution.py:85
  3.1 0.6 %collective-permute-start.2 = (bf16[2,128,128]{2,1,0:T(8,128)(2,1)S(1)}, bf16[2,128,128]{2,1,0:T(8,128)(2,1)S(1)}, u32[]{:S(2)}, u32[]{:S(2)}) collective-permute-start(bf16[2,128,128]{2,1,0:T(8,128)(2,1)S(1)} %get-tuple-element.25), channel_id=1, source_target_pairs={{0,4},{4,0},{8,12},{12,8},{16,20},{20,16},{24,28},{28,24},{1,5},{5... | collective-permute-start | bytes 196616 | tf_op jit(solution)/shard_map/ppermute | solution.py:300
  3.7 1.5 %collective-permute-start = (bf16[2,128,128]{2,1,0:T(8,128)(2,1)S(1)}, bf16[2,128,128]{2,1,0:T(8,128)(2,1)S(1)}, u32[]{:S(2)}, u32[]{:S(2)}) collective-permute-start(bf16[2,128,128]{2,1,0:T(8,128)(2,1)S(1)} %get-tuple-element.26), channel_id=1, source_target_pairs={{0,4},{4,0},{8,12},{12,8},{16,20},{20,16},{24,28},{28,24},{1,5},{5... | collective-permute-start | bytes 196616 | tf_op jit(solution)/shard_map/ppermute | solution.py:301
  5.2 2.5 %collective-permute-done.2.got_ref = bf16[2,128,128]{2,1,0:T(8,128)(2,1)S(1)} collective-permute-done((bf16[2,128,128]{2,1,0:T(8,128)(2,1)S(1)}, bf16[2,128,128]{2,1,0:T(8,128)(2,1)S(1)}, u32[]{:S(2)}, u32[]{:S(2)}) %collective-permute-start.2) | collective-permute-done | bytes 65568 | tf_op jit(solution)/shard_map/ppermute | solution.py:300
  7.7 2.7 %collective-permute-start.3 = (bf16[2,128,128]{2,1,0:T(8,128)(2,1)S(1)}, bf16[2,128,128]{2,1,0:T(8,128)(2,1)S(1)}, u32[]{:S(2)}, u32[]{:S(2)}) collective-permute-start(bf16[2,128,128]{2,1,0:T(8,128)(2,1)S(1)} %get-tuple-element.17), channel_id=1, source_target_pairs={{0,16},{4,20},{8,24},{12,28},{16,0},{20,4},{24,8},{28,12},{1,17},{... | collective-permute-start | bytes 196616 | tf_op jit(solution)/shard_map/ppermute | solution.py:306
  10.3 1.3 %collective-permute-start.4 = (bf16[2,128,128]{2,1,0:T(8,128)(2,1)S(1)}, bf16[2,128,128]{2,1,0:T(8,128)(2,1)S(1)}, u32[]{:S(2)}, u32[]{:S(2)}) collective-permute-start(bf16[2,128,128]{2,1,0:T(8,128)(2,1)S(1)} %get-tuple-element.18), channel_id=1, source_target_pairs={{0,24},{4,28},{8,16},{12,20},{16,8},{20,12},{24,0},{28,4},{1,25},{... | collective-permute-start | bytes 196616 | tf_op jit(solution)/shard_map/ppermute | solution.py:306
  11.7 0.0 collective-permute-done.got_ref
  11.7 0.0 copy-start.4
  11.7 0.3 %collective-permute-start.1 = (bf16[2,128,128]{2,1,0:T(8,128)(2,1)S(1)}, bf16[2,128,128]{2,1,0:T(8,128)(2,1)S(1)}, u32[]{:S(2)}, u32[]{:S(2)}) collective-permute-start(bf16[2,128,128]{2,1,0:T(8,128)(2,1)S(1)} %pairs.2), channel_id=1, source_target_pairs={{0,8},{4,12},{8,0},{12,4},{16,24},{20,28},{24,16},{28,20},{1,9},{5... | collective-permute-start | bytes 196616 | tf_op jit(solution)/shard_map/ppermute | solution.py:306
  12.0 0.0 copy-done.3
  12.0 0.0 collective-permute-start.8
  12.0 0.7 %collective-permute-start.10 = (bf16[1024,128]{1,0:T(8,128)(2,1)S(1)}, bf16[1024,128]{1,0:T(8,128)(2,1)S(1)}, u32[]{:S(2)}, u32[]{:S(2)}) collective-permute-start(bf16[1024,128]{1,0:T(8,128)(2,1)S(1)} %copy-done.3), channel_id=1, source_target_pairs={{3,4},{4,3},{7,8},{8,7},{11,12},{12,11},{15,16},{16,15},{19,20},{2... | collective-permute-start | bytes 786440 | tf_op jit(solution)/shard_map/ppermute | solution.py:293
  12.7 2.2 %collective-permute-done.3.refs_1_ = bf16[2,128,128]{2,1,0:T(8,128)(2,1)S(1)} collective-permute-done((bf16[2,128,128]{2,1,0:T(8,128)(2,1)S(1)}, bf16[2,128,128]{2,1,0:T(8,128)(2,1)S(1)}, u32[]{:S(2)}, u32[]{:S(2)}) %collective-permute-start.3) | collective-permute-done | bytes 65568 | tf_op jit(solution)/shard_map/ppermute | solution.py:306
  14.9 1.9 %collective-permute-start.9 = (bf16[1024,128]{1,0:T(8,128)(2,1)S(1)}, bf16[1024,128]{1,0:T(8,128)(2,1)S(1)}, u32[]{:S(2)}, u32[]{:S(2)}) collective-permute-start(bf16[1024,128]{1,0:T(8,128)(2,1)S(1)} %copy-done.3), channel_id=1, source_target_pairs={{1,2},{2,1},{5,6},{6,5},{9,10},{10,9},{13,14},{14,13},{17,18},{18,... | collective-permute-start | bytes 786440 | tf_op jit(solution)/shard_map/ppermute | solution.py:294
  16.8 0.0 collective-permute-done.4.refs_2_
  16.8 0.0 collective-permute-done.1.refs_0_
  16.8 0.6 %mid.2 = (bf16[128,128]{1,0:T(8,128)(2,1)S(1)}, bf16[128,128]{1,0:T(8,128)(2,1)S(1)}, bf16[2,128,1024]{2,1,0:T(8,128)(2,1)S(1)}) custom-call(bf16[4,128,128]{2,1,0:T(8,128)(2,1)S(1)} %get-tuple-element.15.own_ref, bf16[2,128,128]{2,1,0:T(8,128)(2,1)S(1)} %collective-permute-done.got_ref, bf16[2,128,128]{2,1,0:T(8,128)(2,1)S(1)} %collective-permute-done.1.refs_0_, ...), custom_call_target="tpu_custom_call" | custom-call | flops 134217728 | bytes 1048576 | tf_op jit(solution)/shard_map/mid/pallas_call | solution.py:238
  17.4 0.4 %mid.3 = (bf16[128,128]{1,0:T(8,128)(2,1)S(1)}, bf16[128,128]{1,0:T(8,128)(2,1)S(1)}) custom-call(bf16[2,128,1024]{2,1,0:T(8,128)(2,1)S(1)} %get-tuple-element.21.rhs, bf16[2,512,1024]{2,1,0:T(8,128)(2,1)S(1)} %copy-done), custom_call_target="tpu_custom_call" | custom-call | flops 134217728 | bytes 1048576 | tf_op jit(solution)/shard_map/mid/pallas_call | solution.py:238
  17.9 0.1 collective-permute-start.7
  18.0 0.0 copy-start.2
  18.0 2.1 %collective-permute-start.5 = (bf16[128,128]{1,0:T(8,128)(2,1)S(1)}, bf16[128,128]{1,0:T(8,128)(2,1)S(1)}, u32[]{:S(2)}, u32[]{:S(2)}) collective-permute-start(bf16[128,128]{1,0:T(8,128)(2,1)S(1)} %get-tuple-element.19), channel_id=1, source_target_pairs={{0,2},{1,3},{2,0},{3,1},{4,6},{5,7},{6,4},{7,5},{8,10},{9,11},{10,... | collective-permute-start | bytes 98312 | tf_op jit(solution)/shard_map/ppermute | solution.py:317
  20.1 0.0 collective-permute-done.8.first_ref
  20.1 0.0 collective-permute-start.6
  20.2 0.0 collective-permute-done.10.third_ref
  20.2 5.5 %collective-permute-done.9.second_ref = bf16[1024,128]{1,0:T(8,128)(2,1)S(1)} collective-permute-done((bf16[1024,128]{1,0:T(8,128)(2,1)S(1)}, bf16[1024,128]{1,0:T(8,128)(2,1)S(1)}, u32[]{:S(2)}, u32[]{:S(2)}) %collective-permute-start.9) | collective-permute-done | bytes 262176 | tf_op jit(solution)/shard_map/ppermute | solution.py:294
  25.7 0.0 copy-done.2
  25.7 1.1 %near.1 = (f32[1024,128]{1,0:T(8,128)S(1)}, bf16[3072,128]{1,0:T(8,128)(2,1)S(1)}) custom-call(s32[8,5]{1,0:T(8,128)S(1)} %slots.1.slot_ref, bf16[3072,128]{1,0:T(8,128)(2,1)S(1)} %table.1.table_in, bf16[1024,128]{1,0:T(8,128)(2,1)S(1)} %collective-permute-done.9.second_ref, ...), custom_call_target="tpu_custom_call", output_to_operand_aliasing={{1}: (1, {})} | custom-call | flops 335544320 | bytes 2621440 | tf_op jit(solution)/shard_map/near/pallas_call | solution.py:172
  26.7 0.0 collective-permute-done.7.refs_1_
  26.8 0.5 %far.2.refs_3_ = f32[1024,128]{1,0:T(8,128)S(1)} custom-call(bf16[128,128]{1,0:T(8,128)(2,1)S(1)} %get-tuple-element.22.refs_0_, bf16[128,128]{1,0:T(8,128)(2,1)S(1)} %collective-permute-done.7.refs_1_, bf16[2,1024,512]{2,1,0:T(8,128)(2,1)S(1)} %copy-done.1, f32[1024,128]{1,0:T(8,128)S(1)} %get-tuple-element.24.refs_3_), custom_call_target="tpu_custom_call" | custom-call | flops 134217728 | bytes 1048576 | tf_op jit(solution)/shard_map/far/pallas_call | solution.py:271
  27.3 0.0 collective-permute-done.5.refs_0_
  27.3 0.0 collective-permute-done.6.refs_1_
  27.3 1.2 %far.3 = bf16[1024,128]{1,0:T(8,128)(2,1)} custom-call(bf16[128,128]{1,0:T(8,128)(2,1)S(1)} %collective-permute-done.5.refs_0_, bf16[128,128]{1,0:T(8,128)(2,1)S(1)} %collective-permute-done.6.refs_1_, bf16[2,1024,512]{2,1,0:T(8,128)(2,1)S(1)} %copy-done.1, f32[1024,128]{1,0:T(8,128)S(1)} %far.2.refs_3_), custom_call_target="tpu_custom_call" | custom-call | flops 134217728 | bytes 1048576 | tf_op jit(solution)/shard_map/far/pallas_call | solution.py:271
  (11 shorter events, 0.1 us)
Async XLA Ops:
  0.0 12.0 %copy-start.3 = (bf16[1024,128]{1,0:T(8,128)(2,1)S(1)}, bf16[1024,128]{1,0:T(8,128)(2,1)}, u32[]{:S(2)}) copy-start(bf16[1024,128]{1,0:T(8,128)(2,1)} %own_ref.1) | copy-start | bytes 786436
  0.0 16.8 %copy-start = (bf16[2,512,1024]{2,1,0:T(8,128)(2,1)S(1)}, bf16[2,512,1024]{2,1,0:T(8,128)(2,1)}, u32[]{:S(2)}) copy-start(bf16[2,512,1024]{2,1,0:T(8,128)(2,1)} %c_ref.1) | copy-start | bytes 6291460
  3.1 4.6 %collective-permute-start.2 = (bf16[2,128,128]{2,1,0:T(8,128)(2,1)S(1)}, bf16[2,128,128]{2,1,0:T(8,128)(2,1)S(1)}, u32[]{:S(2)}, u32[]{:S(2)}) collective-permute-start(bf16[2,128,128]{2,1,0:T(8,128)(2,1)S(1)} %get-tuple-element.25), channel_id=1, source_target_pairs={{0,4},{4,0},{8,12},{12,8},{16,20},{20,16},{24,28},{28,24},{1,5},{5... | collective-permute-start | bytes 196616 | tf_op jit(solution)/shard_map/ppermute | solution.py:300
  3.7 8.0 %collective-permute-start = (bf16[2,128,128]{2,1,0:T(8,128)(2,1)S(1)}, bf16[2,128,128]{2,1,0:T(8,128)(2,1)S(1)}, u32[]{:S(2)}, u32[]{:S(2)}) collective-permute-start(bf16[2,128,128]{2,1,0:T(8,128)(2,1)S(1)} %get-tuple-element.26), channel_id=1, source_target_pairs={{0,4},{4,0},{8,12},{12,8},{16,20},{20,16},{24,28},{28,24},{1,5},{5... | collective-permute-start | bytes 196616 | tf_op jit(solution)/shard_map/ppermute | solution.py:301
  7.7 7.2 %collective-permute-start.3 = (bf16[2,128,128]{2,1,0:T(8,128)(2,1)S(1)}, bf16[2,128,128]{2,1,0:T(8,128)(2,1)S(1)}, u32[]{:S(2)}, u32[]{:S(2)}) collective-permute-start(bf16[2,128,128]{2,1,0:T(8,128)(2,1)S(1)} %get-tuple-element.17), channel_id=1, source_target_pairs={{0,16},{4,20},{8,24},{12,28},{16,0},{20,4},{24,8},{28,12},{1,17},{... | collective-permute-start | bytes 196616 | tf_op jit(solution)/shard_map/ppermute | solution.py:306
  10.3 6.5 %collective-permute-start.4 = (bf16[2,128,128]{2,1,0:T(8,128)(2,1)S(1)}, bf16[2,128,128]{2,1,0:T(8,128)(2,1)S(1)}, u32[]{:S(2)}, u32[]{:S(2)}) collective-permute-start(bf16[2,128,128]{2,1,0:T(8,128)(2,1)S(1)} %get-tuple-element.18), channel_id=1, source_target_pairs={{0,24},{4,28},{8,16},{12,20},{16,8},{20,12},{24,0},{28,4},{1,25},{... | collective-permute-start | bytes 196616 | tf_op jit(solution)/shard_map/ppermute | solution.py:306
  11.7 6.3 %copy-start.4 = (s32[8,5]{1,0:T(8,128)S(1)}, s32[8,5]{1,0:T(8,128)}, u32[]{:S(2)}) copy-start(s32[8,5]{1,0:T(8,128)} %list_ref.1) | copy-start | bytes 484
  11.7 5.1 %collective-permute-start.1 = (bf16[2,128,128]{2,1,0:T(8,128)(2,1)S(1)}, bf16[2,128,128]{2,1,0:T(8,128)(2,1)S(1)}, u32[]{:S(2)}, u32[]{:S(2)}) collective-permute-start(bf16[2,128,128]{2,1,0:T(8,128)(2,1)S(1)} %pairs.2), channel_id=1, source_target_pairs={{0,8},{4,12},{8,0},{12,4},{16,24},{20,28},{24,16},{28,20},{1,9},{5... | collective-permute-start | bytes 196616 | tf_op jit(solution)/shard_map/ppermute | solution.py:306
  12.0 8.1 %collective-permute-start.8 = (bf16[1024,128]{1,0:T(8,128)(2,1)S(1)}, bf16[1024,128]{1,0:T(8,128)(2,1)S(1)}, u32[]{:S(2)}, u32[]{:S(2)}) collective-permute-start(bf16[1024,128]{1,0:T(8,128)(2,1)S(1)} %copy-done.3), channel_id=1, source_target_pairs={{0,1},{1,0},{2,3},{3,2},{4,5},{5,4},{6,7},{7,6},{8,9},{9,8},{10,11... | collective-permute-start | bytes 786440 | tf_op jit(solution)/shard_map/ppermute | solution.py:295
  12.0 8.2 %collective-permute-start.10 = (bf16[1024,128]{1,0:T(8,128)(2,1)S(1)}, bf16[1024,128]{1,0:T(8,128)(2,1)S(1)}, u32[]{:S(2)}, u32[]{:S(2)}) collective-permute-start(bf16[1024,128]{1,0:T(8,128)(2,1)S(1)} %copy-done.3), channel_id=1, source_target_pairs={{3,4},{4,3},{7,8},{8,7},{11,12},{12,11},{15,16},{16,15},{19,20},{2... | collective-permute-start | bytes 786440 | tf_op jit(solution)/shard_map/ppermute | solution.py:293
  14.9 10.8 %collective-permute-start.9 = (bf16[1024,128]{1,0:T(8,128)(2,1)S(1)}, bf16[1024,128]{1,0:T(8,128)(2,1)S(1)}, u32[]{:S(2)}, u32[]{:S(2)}) collective-permute-start(bf16[1024,128]{1,0:T(8,128)(2,1)S(1)} %copy-done.3), channel_id=1, source_target_pairs={{1,2},{2,1},{5,6},{6,5},{9,10},{10,9},{13,14},{14,13},{17,18},{18,... | collective-permute-start | bytes 786440 | tf_op jit(solution)/shard_map/ppermute | solution.py:294
  17.9 8.9 %collective-permute-start.7 = (bf16[128,128]{1,0:T(8,128)(2,1)S(1)}, bf16[128,128]{1,0:T(8,128)(2,1)S(1)}, u32[]{:S(2)}, u32[]{:S(2)}) collective-permute-start(bf16[128,128]{1,0:T(8,128)(2,1)S(1)} %get-tuple-element.23), channel_id=1, source_target_pairs={{0,1},{1,0},{2,3},{3,2},{4,5},{5,4},{6,7},{7,6},{8,9},{9,8},{10,11... | collective-permute-start | bytes 98312 | tf_op jit(solution)/shard_map/ppermute | solution.py:317
  18.0 7.7 %copy-start.2 = (bf16[2,1024,640]{2,1,0:T(8,128)(2,1)S(1)}, bf16[2,1024,640]{2,1,0:T(8,128)(2,1)}, u32[]{:S(2)}) copy-start(bf16[2,1024,640]{2,1,0:T(8,128)(2,1)} %p_ref.1) | copy-start | bytes 7864324
  18.0 9.3 %collective-permute-start.5 = (bf16[128,128]{1,0:T(8,128)(2,1)S(1)}, bf16[128,128]{1,0:T(8,128)(2,1)S(1)}, u32[]{:S(2)}, u32[]{:S(2)}) collective-permute-start(bf16[128,128]{1,0:T(8,128)(2,1)S(1)} %get-tuple-element.19), channel_id=1, source_target_pairs={{0,2},{1,3},{2,0},{3,1},{4,6},{5,7},{6,4},{7,5},{8,10},{9,11},{10,... | collective-permute-start | bytes 98312 | tf_op jit(solution)/shard_map/ppermute | solution.py:317
  20.1 6.6 %copy-start.1 = (bf16[2,1024,512]{2,1,0:T(8,128)(2,1)S(1)}, bf16[2,1024,512]{2,1,0:T(8,128)(2,1)}, u32[]{:S(2)}) copy-start(bf16[2,1024,512]{2,1,0:T(8,128)(2,1)} %refs_2_.3) | copy-start | bytes 6291460
  20.1 7.2 %collective-permute-start.6 = (bf16[128,128]{1,0:T(8,128)(2,1)S(1)}, bf16[128,128]{1,0:T(8,128)(2,1)S(1)}, u32[]{:S(2)}, u32[]{:S(2)}) collective-permute-start(bf16[128,128]{1,0:T(8,128)(2,1)S(1)} %get-tuple-element.20), channel_id=1, source_target_pairs={{0,3},{1,2},{2,1},{3,0},{4,7},{5,6},{6,5},{7,4},{8,11},{9,10},{10,... | collective-permute-start | bytes 98312 | tf_op jit(solution)/shard_map/ppermute | solution.py:317

commit v5 on v4

--- a/solution.py
+++ b/solution.py
@@ -142,65 +142,67 @@
     )(own, first)
 
 
-def near_kernel(slot_ref, table_in, second_ref, third_ref, p_ref, o_ref, table, rhs):
-    count = second_ref.shape[0]
+def awaits_edge():
     col = lax.axis_index("col")
+    here = lax.axis_index(("row", "col"))
+    last = lax.axis_size("row") * lax.axis_size("col") - 1
     edge = (col == 0) | (col == lax.axis_size("col") - 1)
-
-    @pl.when(edge)
+    return edge & (here != 0) & (here != last)
+
+
+def near_kernel(late, slot_ref, table_in, side_ref, p_ref, *refs):
+    o_ref, table, rhs = refs[-3:]
+    count = side_ref.shape[0]
+
+    @pl.when(awaits_edge() == late)
     def _():
-        table[2 * count :] = third_ref[...]
-
-    @pl.when(jnp.logical_not(edge))
-    def _():
-        table[2 * count :] = second_ref[...]
-
-    slots = slot_ref[...] * LEAF
-    for i in range(count // LEAF):
-        rows = slice(i * LEAF, (i + 1) * LEAF)
-        for j in range(NEAR):
-            at = pl.ds(pl.multiple_of(slots[i, j], LEAF), LEAF)
-            rhs[i % 2, j * LEAF : (j + 1) * LEAF] = table[at]
-        data = rhs[i % 2]
-        straight = dot(p_ref[0, rows], data)
-        crossed = dot(p_ref[1, rows], data)
-        o_ref[rows] = straight + turn_lanes(crossed)
-
-
-def near(slots, table, second, third, blocks):
-    count, width = second.shape
-    return pl.pallas_call(
-        near_kernel,
+        table[2 * count :] = side_ref[...]
+        slots = slot_ref[...] * LEAF
+        for i in range(count // LEAF):
+            rows = slice(i * LEAF, (i + 1) * LEAF)
+            for j in range(NEAR):
+                at = pl.ds(pl.multiple_of(slots[i, j], LEAF), LEAF)
+                rhs[i % 2, j * LEAF : (j + 1) * LEAF] = table[at]
+            data = rhs[i % 2]
+            straight = dot(p_ref[0, rows], data)
+            crossed = dot(p_ref[1, rows], data)
+            o_ref[rows] = straight + turn_lanes(crossed)
+
+
+def near(late, slots, table, side, blocks, *total):
+    count, width = side.shape
+    return pl.pallas_call(
+        functools.partial(near_kernel, late),
         out_shape=[
             jax.ShapeDtypeStruct((count, width), jnp.float32),
             jax.ShapeDtypeStruct(table.shape, table.dtype),
         ],
-        in_specs=[VMEM] * 5,
+        in_specs=[VMEM] * (4 + len(total)),
         out_specs=[VMEM, VMEM],
-        input_output_aliases={1: 1},
+        input_output_aliases={1: 1, 4: 0} if total else {1: 1},
         scratch_shapes=[pltpu.VMEM((2, NEAR * LEAF, width), jnp.bfloat16)],
         compiler_params=params(4),
         cost_estimate=cost(4 * width * blocks.shape[1] * blocks.shape[2], blocks.size * 2),
-        name="near",
-    )(slots, table, second, third, blocks)[0]
-
-
-def pack_kernel(hops, own_ref, got_ref, *outs):
-    base = hops[-1] + 1 - got_ref.shape[0]
-    for k, o_ref in zip(hops, outs):
-        o_ref[0] = own_ref[k]
-        o_ref[1] = got_ref[k - base]
-
-
-def pack(hops, own, got):
-    return pl.pallas_call(
-        functools.partial(pack_kernel, hops),
-        out_shape=[jax.ShapeDtypeStruct((2, *own.shape[1:]), own.dtype)] * len(hops),
+        name="blocks",
+    )(slots, table, side, blocks, *total)
+
+
+def pack_kernel(own_ref, got_ref, *outs):
+    for k, o_ref in enumerate(outs):
+        o_ref[0] = own_ref[k + 1]
+        o_ref[1] = got_ref[k + 1]
+
+
+def pack(own, got):
+    count = own.shape[0] - 1
+    return pl.pallas_call(
+        pack_kernel,
+        out_shape=[jax.ShapeDtypeStruct((2, *own.shape[1:]), own.dtype)] * count,
         in_specs=[VMEM, VMEM],
-        out_specs=[VMEM] * len(hops),
+        out_specs=[VMEM] * count,
         compiler_params=params(1),
-        cost_estimate=cost(0, len(hops) * own.size * 2),
-        name="pairs",
+        cost_estimate=cost(0, own.size * 8),
+        name="pack",
     )(own, got)
 
 
@@ -247,7 +249,7 @@
 
 
 def far_kernel(hops, *refs):
-    landed, (u_ref, n_ref, o_ref, data) = refs[: len(hops)], refs[len(hops) :]
+    landed, u_ref, addends, (o_ref, data) = refs[: len(hops)], refs[len(hops)], refs[len(hops) + 1 : -2], refs[-2:]
     me = lax.axis_index("col")
     for n, k in enumerate(hops):
         at = pl.ds(pl.multiple_of((n & ~1) * RANK + ((me ^ k) & 1) * RANK, RANK), RANK)
@@ -255,29 +257,29 @@
         data[0, at] = value
         data[1, at] = turn_lanes(value.astype(jnp.float32)).astype(jnp.bfloat16)
     step = 2 * RANK
-    for i in range(0, n_ref.shape[0], step):
+    for i in range(0, o_ref.shape[0], step):
         rows = slice(i, i + step)
-        total = n_ref[rows]
+        terms = [ref[rows] for ref in addends]
         for n in range(0, len(hops), 2):
             lanes = pl.ds(pl.multiple_of(((me ^ hops[n]) & ~1) * RANK, 2 * RANK), 2 * RANK)
             at = slice(n * RANK, (n + 2) * RANK)
-            total += dot(u_ref[0, rows, lanes], data[0, at]) + dot(u_ref[1, rows, lanes], data[1, at])
-        o_ref[rows] = total.astype(o_ref.dtype)
-
-
-def far(hops, landed, factors, near_field, kind):
-    count, width = near_field.shape
+            terms.append(dot(u_ref[0, rows, lanes], data[0, at]) + dot(u_ref[1, rows, lanes], data[1, at]))
+        o_ref[rows] = sum(terms[1:], terms[0]).astype(o_ref.dtype)
+
+
+def far(hops, landed, factors, addends, kind):
+    count, width = factors.shape[1], landed[0].shape[1]
     share = len(hops) * RANK * count
     return pl.pallas_call(
         functools.partial(far_kernel, hops),
         out_shape=jax.ShapeDtypeStruct((count, width), kind),
-        in_specs=[VMEM] * (len(hops) + 2),
+        in_specs=[VMEM] * (len(hops) + 1 + len(addends)),
         out_specs=VMEM,
         scratch_shapes=[pltpu.VMEM((2, len(hops) * RANK, width), jnp.bfloat16)],
         compiler_params=params(4),
         cost_estimate=cost(4 * width * share, share * 4),
         name="far",
-    )(*landed, factors, near_field)
+    )(*landed, factors, *addends)
 
 
 def stages(excitation, near_list, near_blocks, col_factors, coupling, row_factors):
@@ -294,18 +296,14 @@
     second = lax.ppermute(excitation, axes, outer)
     first = lax.ppermute(excitation, axes, inner)
     own, cross = project(excitation, col_factors)
-    steps = row_count // 2
-    beyond, close = list(range(steps // 2, steps)), list(range(1, steps // 2))
-    aside = [(i, i ^ 1) for i in range(row_count)]
-    got_beyond = lax.ppermute(cross[steps // 2 :], "row", aside)
-    got = lax.ppermute(cross[: steps // 2], "row", aside)
-    sent = dict(zip(beyond, pack(beyond, own, got_beyond)))
-    sent.update(zip(close, pack(close, own, got)))
+    got = lax.ppermute(cross, "row", [(i, i ^ 1) for i in range(row_count)])
+    sent = pack(own, got)
     arrived = []
-    for k in range(1, steps):
-        arrived.append(lax.ppermute(sent[k], "row", [(i, i ^ (2 * k)) for i in range(row_count)]))
+    for k in range(1, row_count // 2):
+        arrived.append(lax.ppermute(sent[k - 1], "row", [(i, i ^ (2 * k)) for i in range(row_count)]))
     slots = slots_of(near_list)
     table = table_of(excitation, first)
+    total, table = near(False, slots, table, second, near_blocks)
     early = list(range(2, col_count))
     late = [1, 0]
     turned = jax.ShapeDtypeStruct((2, own.shape[1], coupling.shape[2]), own.dtype)
@@ -315,9 +313,9 @@
     landed = {0: sent[0]}
     for k in reversed(range(1, col_count)):
         landed[k] = lax.ppermute(sent[k], "col", [(i, i ^ k) for i in range(col_count)])
-    total = near(slots, table, second, third, near_blocks)
-    total = far([0, 1], [landed[0], landed[1]], row_factors, total, jnp.float32)
-    return far(early, [landed[k] for k in early], row_factors, total, jnp.bfloat16)
+    partial = far([0, 1], [landed[0], landed[1]], row_factors, [], jnp.float32)
+    total, _ = near(True, slots, table, third, near_blocks, total)
+    return far(early, [landed[k] for k in early], row_factors, [partial, total], jnp.bfloat16)
 
 
 def solution(mesh):

time: 28.7 us -> 27.9 us (0.972)
  the two profiles are of different devices: /device:TPU:6 before, /device:TPU:0 now
where the time goes in v5:
time: 27.9 us; the launch traced here: 27.5 us
  starting transfers between devices  11.4 us (41%)
  waiting for transfers between devices  8.97 us (32%)
  Pallas kernels  6.93 us (25%)
    ppermute x3, waiting for transfers between devices, stages(): lax.ppermute(sent[k - 1], 'row', [(i, i ^ 2 * k) for i in range(row_count)])  4.67 us
    ppermute x3, starting transfers between devices, stages(): lax.ppermute(sent[k - 1], 'row', [(i, i ^ 2 * k) for i in range(row_count)])  4.48 us
    ppermute x1, waiting for transfers between devices, stages(): got = lax.ppermute(cross, 'row', [(i, i ^ 1) for i in range(row_count)])  3.49 us
    ppermute x1, starting transfers between devices, stages(): got = lax.ppermute(cross, 'row', [(i, i ^ 1) for i in range(row_count)])  3.04 us
    pallas_call x1, Pallas kernels, project(): pl.pallas_call(project_kernel, out_shape=[jax.ShapeDtypeStruct((groups //...  3.03 us
    ppermute x3, starting transfers between devices, stages(): lax.ppermute(sent[k], 'col', [(i, i ^ k) for i in range(col_count)])  2.49 us
    pallas_call x2, Pallas kernels, far(): pl.pallas_call(functools.partial(far_kernel, hops), out_shape=jax.ShapeDt...  1.73 us
    pallas_call x2, Pallas kernels, near(): pl.pallas_call(functools.partial(near_kernel, late), out_shape=[jax.Shape...  1.08 us
  transfers between devices with their start and end apart: 10, of which 4 were waited for; matrix products, arithmetic and copies ran while one was open for 0% of the time, Pallas kernels for 10%

profile of v5, /device:TPU:0, one launch (start us, length us, event | category | flops | bytes accessed | tf_op | source)
XLA Modules:
  0.0 27.5 jit_solution(16804974646085153578)
XLA Ops:
  0.0 3.0 %project.1 = (bf16[4,128,128]{2,1,0:T(8,128)(2,1)S(1)}, bf16[4,128,128]{2,1,0:T(8,128)(2,1)S(1)}) custom-call(bf16[1024,128]{1,0:T(8,128)(2,1)} %own_ref.1, bf16[2,1024,1024]{2,1,0:T(8,128)(2,1)} %v_hbm.1), custom_call_target="tpu_custom_call" | custom-call | flops 536870912 | bytes 4194304 | tf_op jit(solution)/shard_map/project/pallas_call | solution.py:85
  3.0 3.0 %collective-permute-start = (bf16[4,128,128]{2,1,0:T(8,128)(2,1)S(1)}, bf16[4,128,128]{2,1,0:T(8,128)(2,1)S(1)}, u32[]{:S(2)}, u32[]{:S(2)}) collective-permute-start(bf16[4,128,128]{2,1,0:T(8,128)(2,1)S(1)} %get-tuple-element.19), channel_id=1, source_target_pairs={{0,4},{4,0},{8,12},{12,8},{16,20},{20,16},{24,28},{28,24},{1,5},{5... | collective-permute-start | bytes 393224 | tf_op jit(solution)/shard_map/ppermute | solution.py:299
  6.1 3.5 %collective-permute-done.got_ref = bf16[4,128,128]{2,1,0:T(8,128)(2,1)S(1)} collective-permute-done((bf16[4,128,128]{2,1,0:T(8,128)(2,1)S(1)}, bf16[4,128,128]{2,1,0:T(8,128)(2,1)S(1)}, u32[]{:S(2)}, u32[]{:S(2)}) %collective-permute-start) | collective-permute-done | bytes 131104 | tf_op jit(solution)/shard_map/ppermute | solution.py:299
  9.6 0.0 copy-start.4
  9.6 1.9 %collective-permute-start.1 = (bf16[2,128,128]{2,1,0:T(8,128)(2,1)S(1)}, bf16[2,128,128]{2,1,0:T(8,128)(2,1)S(1)}, u32[]{:S(2)}, u32[]{:S(2)}) collective-permute-start(bf16[2,128,128]{2,1,0:T(8,128)(2,1)S(1)} %get-tuple-element.20), channel_id=1, source_target_pairs={{0,8},{4,12},{8,0},{12,4},{16,24},{20,28},{24,16},{28,20},{1,9},{5... | collective-permute-start | bytes 196616 | tf_op jit(solution)/shard_map/ppermute | solution.py:303
  11.5 2.6 %collective-permute-start.2 = (bf16[2,128,128]{2,1,0:T(8,128)(2,1)S(1)}, bf16[2,128,128]{2,1,0:T(8,128)(2,1)S(1)}, u32[]{:S(2)}, u32[]{:S(2)}) collective-permute-start(bf16[2,128,128]{2,1,0:T(8,128)(2,1)S(1)} %get-tuple-element.21), channel_id=1, source_target_pairs={{0,16},{4,20},{8,24},{12,28},{16,0},{20,4},{24,8},{28,12},{1,17},{... | collective-permute-start | bytes 196616 | tf_op jit(solution)/shard_map/ppermute | solution.py:303
  14.1 0.0 collective-permute-start.3
  14.1 0.0 copy-done.3
  14.1 0.0 collective-permute-start.7
  14.1 0.7 %collective-permute-start.9 = (bf16[1024,128]{1,0:T(8,128)(2,1)S(1)}, bf16[1024,128]{1,0:T(8,128)(2,1)S(1)}, u32[]{:S(2)}, u32[]{:S(2)}) collective-permute-start(bf16[1024,128]{1,0:T(8,128)(2,1)S(1)} %copy-done.3), channel_id=1, source_target_pairs={{3,4},{4,3},{7,8},{8,7},{11,12},{12,11},{15,16},{16,15},{19,20},{2... | collective-permute-start | bytes 786440 | tf_op jit(solution)/shard_map/ppermute | solution.py:295
  14.8 0.0 collective-permute-done.1.refs_0_
  14.8 0.7 %collective-permute-start.8 = (bf16[1024,128]{1,0:T(8,128)(2,1)S(1)}, bf16[1024,128]{1,0:T(8,128)(2,1)S(1)}, u32[]{:S(2)}, u32[]{:S(2)}) collective-permute-start(bf16[1024,128]{1,0:T(8,128)(2,1)S(1)} %copy-done.3), channel_id=1, source_target_pairs={{1,2},{2,1},{5,6},{6,5},{9,10},{10,9},{13,14},{14,13},{17,18},{18,... | collective-permute-start | bytes 786440 | tf_op jit(solution)/shard_map/ppermute | solution.py:296
  15.5 2.6 %collective-permute-done.2.refs_1_ = bf16[2,128,128]{2,1,0:T(8,128)(2,1)S(1)} collective-permute-done((bf16[2,128,128]{2,1,0:T(8,128)(2,1)S(1)}, bf16[2,128,128]{2,1,0:T(8,128)(2,1)S(1)}, u32[]{:S(2)}, u32[]{:S(2)}) %collective-permute-start.2) | collective-permute-done | bytes 65568 | tf_op jit(solution)/shard_map/ppermute | solution.py:303
  18.1 2.1 %collective-permute-done.3.refs_2_ = bf16[2,128,128]{2,1,0:T(8,128)(2,1)S(1)} collective-permute-done((bf16[2,128,128]{2,1,0:T(8,128)(2,1)S(1)}, bf16[2,128,128]{2,1,0:T(8,128)(2,1)S(1)}, u32[]{:S(2)}, u32[]{:S(2)}) %collective-permute-start.3) | collective-permute-done | bytes 65568 | tf_op jit(solution)/shard_map/ppermute | solution.py:303
  20.1 0.0 copy-done.1
  20.1 0.6 %mid.2 = (bf16[128,128]{1,0:T(8,128)(2,1)S(1)}, bf16[128,128]{1,0:T(8,128)(2,1)S(1)}, bf16[2,128,1024]{2,1,0:T(8,128)(2,1)S(1)}) custom-call(bf16[4,128,128]{2,1,0:T(8,128)(2,1)S(1)} %get-tuple-element.18.own_ref, bf16[4,128,128]{2,1,0:T(8,128)(2,1)S(1)} %collective-permute-done.got_ref, bf16[2,128,128]{2,1,0:T(8,128)(2,1)S(1)} %collective-permute-done.1.refs_0_, ...), custom_call_target="tpu_custom_call" | custom-call | flops 134217728 | bytes 1048576 | tf_op jit(solution)/shard_map/mid/pallas_call | solution.py:240
  20.7 0.4 %mid.3 = (bf16[128,128]{1,0:T(8,128)(2,1)S(1)}, bf16[128,128]{1,0:T(8,128)(2,1)S(1)}) custom-call(bf16[2,128,1024]{2,1,0:T(8,128)(2,1)S(1)} %get-tuple-element.25.rhs, bf16[2,512,1024]{2,1,0:T(8,128)(2,1)S(1)} %copy-done.1), custom_call_target="tpu_custom_call" | custom-call | flops 134217728 | bytes 1048576 | tf_op jit(solution)/shard_map/mid/pallas_call | solution.py:240
  21.2 0.0 copy-start.2
  21.2 0.1 collective-permute-start.6
  21.3 0.0 copy-done.4
  21.3 0.0 copy-start
  21.3 1.6 %collective-permute-start.4 = (bf16[128,128]{1,0:T(8,128)(2,1)S(1)}, bf16[128,128]{1,0:T(8,128)(2,1)S(1)}, u32[]{:S(2)}, u32[]{:S(2)}) collective-permute-start(bf16[128,128]{1,0:T(8,128)(2,1)S(1)} %get-tuple-element.23), channel_id=1, source_target_pairs={{0,2},{1,3},{2,0},{3,1},{4,6},{5,7},{6,4},{7,5},{8,10},{9,11},{10,... | collective-permute-start | bytes 98312 | tf_op jit(solution)/shard_map/ppermute | solution.py:315
  22.9 0.0 collective-permute-done.6.refs_1_
  22.9 0.8 %collective-permute-start.5 = (bf16[128,128]{1,0:T(8,128)(2,1)S(1)}, bf16[128,128]{1,0:T(8,128)(2,1)S(1)}, u32[]{:S(2)}, u32[]{:S(2)}) collective-permute-start(bf16[128,128]{1,0:T(8,128)(2,1)S(1)} %get-tuple-element.24), channel_id=1, source_target_pairs={{0,3},{1,2},{2,1},{3,0},{4,7},{5,6},{6,5},{7,4},{8,11},{9,10},{10,... | collective-permute-start | bytes 98312 | tf_op jit(solution)/shard_map/ppermute | solution.py:315
  23.8 0.5 %far.2.refs_3_ = f32[1024,128]{1,0:T(8,128)S(1)} custom-call(bf16[128,128]{1,0:T(8,128)(2,1)S(1)} %get-tuple-element.26.refs_0_, bf16[128,128]{1,0:T(8,128)(2,1)S(1)} %collective-permute-done.6.refs_1_, bf16[2,1024,512]{2,1,0:T(8,128)(2,1)S(1)} %copy-done.2), custom_call_target="tpu_custom_call" | custom-call | flops 134217728 | bytes 1048576 | tf_op jit(solution)/shard_map/far/pallas_call | solution.py:273
  24.3 0.0 collective-permute-done.7.first_ref
  24.3 0.0 collective-permute-done.8.side_ref
  24.3 1.1 %blocks.2 = (f32[1024,128]{1,0:T(8,128)S(1)}, bf16[3072,128]{1,0:T(8,128)(2,1)S(1)}) custom-call(s32[8,5]{1,0:T(8,128)S(1)} %slots.1.slot_ref, bf16[3072,128]{1,0:T(8,128)(2,1)S(1)} %table.1.table_in, bf16[1024,128]{1,0:T(8,128)(2,1)S(1)} %collective-permute-done.8.side_ref, bf16[2,1024,640]{2,1,0:T(8,128)(2,1)S(1)} %copy-done), custom_call_target="tpu_custom_call", output_to_operand_aliasing={{1}: (1, {})} | custom-call | flops 335544320 | bytes 2621440 | tf_op jit(solution)/shard_map/blocks/pallas_call | solution.py:174
  25.4 0.0 collective-permute-done.9.side_ref
  25.4 0.0 collective-permute-done.4.refs_0_
  25.5 0.8 %collective-permute-done.5.refs_1_ = bf16[128,128]{1,0:T(8,128)(2,1)S(1)} collective-permute-done((bf16[128,128]{1,0:T(8,128)(2,1)S(1)}, bf16[128,128]{1,0:T(8,128)(2,1)S(1)}, u32[]{:S(2)}, u32[]{:S(2)}) %collective-permute-start.5) | collective-permute-done | bytes 32800 | tf_op jit(solution)/shard_map/ppermute | solution.py:315
  26.2 1.2 %far.3 = bf16[1024,128]{1,0:T(8,128)(2,1)} custom-call(bf16[128,128]{1,0:T(8,128)(2,1)S(1)} %collective-permute-done.4.refs_0_, bf16[128,128]{1,0:T(8,128)(2,1)S(1)} %collective-permute-done.5.refs_1_, bf16[2,1024,512]{2,1,0:T(8,128)(2,1)S(1)} %copy-done.2, f32[1024,128]{1,0:T(8,128)S(1)} %far.2.refs_3_, f32[1024,128]{1,0:T(8,128)S(1)} %get-tuple-element.30.refs_4_), custom_call_target="tpu_custom_call" | custom-call | flops 134217728 | bytes 1048576 | tf_op jit(solution)/shard_map/far/pallas_call | solution.py:273
  (8 shorter events, 0.1 us)
Async XLA Ops:
  0.0 14.1 %copy-start.3 = (bf16[1024,128]{1,0:T(8,128)(2,1)S(1)}, bf16[1024,128]{1,0:T(8,128)(2,1)}, u32[]{:S(2)}) copy-start(bf16[1024,128]{1,0:T(8,128)(2,1)} %own_ref.1) | copy-start | bytes 786436
  0.0 20.1 %copy-start.1 = (bf16[2,512,1024]{2,1,0:T(8,128)(2,1)S(1)}, bf16[2,512,1024]{2,1,0:T(8,128)(2,1)}, u32[]{:S(2)}) copy-start(bf16[2,512,1024]{2,1,0:T(8,128)(2,1)} %c_ref.1) | copy-start | bytes 6291460
  3.0 6.5 %collective-permute-start = (bf16[4,128,128]{2,1,0:T(8,128)(2,1)S(1)}, bf16[4,128,128]{2,1,0:T(8,128)(2,1)S(1)}, u32[]{:S(2)}, u32[]{:S(2)}) collective-permute-start(bf16[4,128,128]{2,1,0:T(8,128)(2,1)S(1)} %get-tuple-element.19), channel_id=1, source_target_pairs={{0,4},{4,0},{8,12},{12,8},{16,20},{20,16},{24,28},{28,24},{1,5},{5... | collective-permute-start | bytes 393224 | tf_op jit(solution)/shard_map/ppermute | solution.py:299
  9.6 11.7 %copy-start.4 = (s32[8,5]{1,0:T(8,128)S(1)}, s32[8,5]{1,0:T(8,128)}, u32[]{:S(2)}) copy-start(s32[8,5]{1,0:T(8,128)} %list_ref.1) | copy-start | bytes 484
  9.6 5.2 %collective-permute-start.1 = (bf16[2,128,128]{2,1,0:T(8,128)(2,1)S(1)}, bf16[2,128,128]{2,1,0:T(8,128)(2,1)S(1)}, u32[]{:S(2)}, u32[]{:S(2)}) collective-permute-start(bf16[2,128,128]{2,1,0:T(8,128)(2,1)S(1)} %get-tuple-element.20), channel_id=1, source_target_pairs={{0,8},{4,12},{8,0},{12,4},{16,24},{20,28},{24,16},{28,20},{1,9},{5... | collective-permute-start | bytes 196616 | tf_op jit(solution)/shard_map/ppermute | solution.py:303
  11.5 6.6 %collective-permute-start.2 = (bf16[2,128,128]{2,1,0:T(8,128)(2,1)S(1)}, bf16[2,128,128]{2,1,0:T(8,128)(2,1)S(1)}, u32[]{:S(2)}, u32[]{:S(2)}) collective-permute-start(bf16[2,128,128]{2,1,0:T(8,128)(2,1)S(1)} %get-tuple-element.21), channel_id=1, source_target_pairs={{0,16},{4,20},{8,24},{12,28},{16,0},{20,4},{24,8},{28,12},{1,17},{... | collective-permute-start | bytes 196616 | tf_op jit(solution)/shard_map/ppermute | solution.py:303
  14.1 6.1 %collective-permute-start.3 = (bf16[2,128,128]{2,1,0:T(8,128)(2,1)S(1)}, bf16[2,128,128]{2,1,0:T(8,128)(2,1)S(1)}, u32[]{:S(2)}, u32[]{:S(2)}) collective-permute-start(bf16[2,128,128]{2,1,0:T(8,128)(2,1)S(1)} %get-tuple-element.22), channel_id=1, source_target_pairs={{0,24},{4,28},{8,16},{12,20},{16,8},{20,12},{24,0},{28,4},{1,25},{... | collective-permute-start | bytes 196616 | tf_op jit(solution)/shard_map/ppermute | solution.py:303
  14.1 10.2 %collective-permute-start.7 = (bf16[1024,128]{1,0:T(8,128)(2,1)S(1)}, bf16[1024,128]{1,0:T(8,128)(2,1)S(1)}, u32[]{:S(2)}, u32[]{:S(2)}) collective-permute-start(bf16[1024,128]{1,0:T(8,128)(2,1)S(1)} %copy-done.3), channel_id=1, source_target_pairs={{0,1},{1,0},{2,3},{3,2},{4,5},{5,4},{6,7},{7,6},{8,9},{9,8},{10,11... | collective-permute-start | bytes 786440 | tf_op jit(solution)/shard_map/ppermute | solution.py:297
  14.1 11.3 %collective-permute-start.9 = (bf16[1024,128]{1,0:T(8,128)(2,1)S(1)}, bf16[1024,128]{1,0:T(8,128)(2,1)S(1)}, u32[]{:S(2)}, u32[]{:S(2)}) collective-permute-start(bf16[1024,128]{1,0:T(8,128)(2,1)S(1)} %copy-done.3), channel_id=1, source_target_pairs={{3,4},{4,3},{7,8},{8,7},{11,12},{12,11},{15,16},{16,15},{19,20},{2... | collective-permute-start | bytes 786440 | tf_op jit(solution)/shard_map/ppermute | solution.py:295
  14.8 9.5 %collective-permute-start.8 = (bf16[1024,128]{1,0:T(8,128)(2,1)S(1)}, bf16[1024,128]{1,0:T(8,128)(2,1)S(1)}, u32[]{:S(2)}, u32[]{:S(2)}) collective-permute-start(bf16[1024,128]{1,0:T(8,128)(2,1)S(1)} %copy-done.3), channel_id=1, source_target_pairs={{1,2},{2,1},{5,6},{6,5},{9,10},{10,9},{13,14},{14,13},{17,18},{18,... | collective-permute-start | bytes 786440 | tf_op jit(solution)/shard_map/ppermute | solution.py:296
  21.2 2.6 %copy-start.2 = (bf16[2,1024,512]{2,1,0:T(8,128)(2,1)S(1)}, bf16[2,1024,512]{2,1,0:T(8,128)(2,1)}, u32[]{:S(2)}) copy-start(bf16[2,1024,512]{2,1,0:T(8,128)(2,1)} %refs_2_.3) | copy-start | bytes 6291460
  21.2 1.7 %collective-permute-start.6 = (bf16[128,128]{1,0:T(8,128)(2,1)S(1)}, bf16[128,128]{1,0:T(8,128)(2,1)S(1)}, u32[]{:S(2)}, u32[]{:S(2)}) collective-permute-start(bf16[128,128]{1,0:T(8,128)(2,1)S(1)} %get-tuple-element.27), channel_id=1, source_target_pairs={{0,1},{1,0},{2,3},{3,2},{4,5},{5,4},{6,7},{7,6},{8,9},{9,8},{10,11... | collective-permute-start | bytes 98312 | tf_op jit(solution)/shard_map/ppermute | solution.py:315
  21.3 3.0 %copy-start = (bf16[2,1024,640]{2,1,0:T(8,128)(2,1)S(1)}, bf16[2,1024,640]{2,1,0:T(8,128)(2,1)}, u32[]{:S(2)}) copy-start(bf16[2,1024,640]{2,1,0:T(8,128)(2,1)} %p_ref.3) | copy-start | bytes 7864324
  21.3 4.1 %collective-permute-start.4 = (bf16[128,128]{1,0:T(8,128)(2,1)S(1)}, bf16[128,128]{1,0:T(8,128)(2,1)S(1)}, u32[]{:S(2)}, u32[]{:S(2)}) collective-permute-start(bf16[128,128]{1,0:T(8,128)(2,1)S(1)} %get-tuple-element.23), channel_id=1, source_target_pairs={{0,2},{1,3},{2,0},{3,1},{4,6},{5,7},{6,4},{7,5},{8,10},{9,11},{10,... | collective-permute-start | bytes 98312 | tf_op jit(solution)/shard_map/ppermute | solution.py:315
  22.9 3.3 %collective-permute-start.5 = (bf16[128,128]{1,0:T(8,128)(2,1)S(1)}, bf16[128,128]{1,0:T(8,128)(2,1)S(1)}, u32[]{:S(2)}, u32[]{:S(2)}) collective-permute-start(bf16[128,128]{1,0:T(8,128)(2,1)S(1)} %get-tuple-element.24), channel_id=1, source_target_pairs={{0,3},{1,2},{2,1},{3,0},{4,7},{5,6},{6,5},{7,4},{8,11},{9,10},{10,... | collective-permute-start | bytes 98312 | tf_op jit(solution)/shard_map/ppermute | solution.py:315
